TPU v7x, 512 devices: a whole 4x8x8 slice. The times are simulated.
512 devices in a mesh: tm: 64 (over z, y), rhs: 8 (over x, core).
Axes of the slice: x: 4, y: 8, z: 8, core: 2. Of those that a mesh axis runs over, the one named last changes fastest.
Arguments:
- jacobians: bfloat16 [128, 256, 256], P('tm', 'rhs'), may hold values from -0.065625 to 0.065625, as said below
- damping: float32 [128, 256], P('tm'), may hold values from 0.003 to 0.008
- right_sides: float32 [64, 128, 256], P('rhs', 'tm'), may hold values from -0.8 to 0.8, as said below
Outputs:
- solution: float32 [64, 128, 256], P('rhs', 'tm')
Inputs may be any that keep to these rules, and one draw needn't show every extreme that they name: `jacobians`: real values of both signs. `right_sides`: real values, rough from section to section.
All inputs are finite; a program needn't handle non-finite values.
Results may differ from a plain program's by a relative error of at most 0.0003.
Values may be sent and summed in bfloat16 or wider, within the bound.
A program may use at most 128 MiB of HBM per device.

v0:
```python
import jax
import jax.numpy as jnp
from jax import lax
from jax.sharding import PartitionSpec as P

HIGHEST = lax.Precision.HIGHEST


def passed_along(value, axis, by):
    length = lax.axis_size(axis)
    pairs = [(i, i + by) for i in range(length) if 0 <= i + by < length]
    return lax.ppermute(value, axis, pairs)


def lower_solve(factor, values):
    return lax.linalg.triangular_solve(factor, values, left_side=True, lower=True)


def upper_solve(factor, values):
    return lax.linalg.triangular_solve(factor, values, left_side=True, lower=True, transpose_a=True)


def tproduct(former, latter):
    return jnp.dot(former.T, latter, precision=HIGHEST, preferred_element_type=jnp.float32)


def mproduct(former, latter):
    return jnp.dot(former, latter, precision=HIGHEST, preferred_element_type=jnp.float32)


def blocks_along(package, stride):
    return passed_along(package, "tm", stride)


def values_along(solved, stride):
    return passed_along(solved, "tm", stride)


def add_rows(row_piece):
    gram_sum = jnp.einsum("kab,kac->kbc", row_piece, row_piece, preferred_element_type=jnp.float32)
    return (gram_sum, row_piece)


def eliminate(operands):
    reduced_diag, reduced_low, reduced_up, reduced_rhs = operands
    factor = jnp.linalg.cholesky(reduced_diag)
    return (
        factor,
        lower_solve(factor, reduced_low),
        lower_solve(factor, reduced_up),
        lower_solve(factor, reduced_rhs),
    )


def pass_over(operands):
    reduced_diag, reduced_low, reduced_up, reduced_rhs = operands
    identity = jnp.eye(reduced_diag.shape[0], dtype=jnp.float32)
    return (
        identity,
        jnp.zeros_like(reduced_low),
        jnp.zeros_like(reduced_up),
        jnp.zeros_like(reduced_rhs),
    )


def owner_terms(operands):
    w_low, w_up, w_rhs = operands
    cross = tproduct(w_low, w_up)
    below_terms = (tproduct(w_low, w_low), -cross, tproduct(w_low, w_rhs))
    above_terms = (tproduct(w_up, w_up), -cross.T, tproduct(w_up, w_rhs))
    return (below_terms, above_terms)


def no_terms(operands):
    w_low, w_up, w_rhs = operands
    zero_block = jnp.zeros_like(w_low)
    zero_rhs = jnp.zeros_like(w_rhs)
    return ((zero_block, zero_block, zero_rhs), (zero_block, zero_block, zero_rhs))


def root_solve(operands):
    reduced_diag, reduced_rhs = operands
    factor = jnp.linalg.cholesky(reduced_diag)
    return upper_solve(factor, lower_solve(factor, reduced_rhs))


def root_skip(operands):
    reduced_diag, reduced_rhs = operands
    return jnp.zeros_like(reduced_rhs)


def per_device(jacobians, damping, right_sides):
    sections = jacobians.shape[0]
    state_width = jacobians.shape[2]
    device_count = lax.axis_size("tm")
    position = lax.axis_index("tm")
    identity = jnp.eye(state_width, dtype=jnp.float32)
    gram_sum, whole = add_rows(lax.all_gather(jacobians, "rhs", axis=1, tiled=True))
    section_ids = position * sections + jnp.arange(sections, dtype=jnp.int32)
    later_section = (section_ids > 0).astype(jnp.float32)
    hess_blocks = (
        gram_sum
        + damping[:, :, None] * identity[None]
        + later_section[:, None, None] * identity[None]
    )
    link_mask = (section_ids < sections * device_count - 1).astype(jnp.float32)
    couplings = -jnp.swapaxes(whole, 1, 2).astype(jnp.float32) * link_mask[:, None, None]
    columns = jnp.transpose(right_sides, (1, 2, 0))
    spikes_full = []
    link_prev = None
    column_list = []
    offset = 1
    hess_block = hess_blocks[offset]
    spike_rhs = jnp.zeros((state_width, 2 * state_width), jnp.float32)
    spike_rhs = spike_rhs.at[:, :state_width].set(-whole[0].astype(jnp.float32))
    spike_rhs = spike_rhs.at[:, state_width:].set(couplings[sections - 1])
    column = columns[offset]
    factor = jnp.linalg.cholesky(hess_block)
    spike_now = lower_solve(factor, spike_rhs)
    column_now = lower_solve(factor, column)
    total = tproduct(spike_now, spike_now)
    total_rhs = tproduct(spike_now, column_now)
    spike_list = [spike_now]
    column_list.append(column_now)
    link_prev = None
    interior = [(factor, column_now, link_prev)]
    spikes_full = spike_list
    reduced_up = -total[:state_width, state_width:]
    package = (total[state_width:, state_width:], reduced_up, total_rhs[state_width:])
    reduced_diag = hess_blocks[0] - total[:state_width, :state_width]
    reduced_rhs = columns[0] - total_rhs[:state_width]
    prev_diag, prev_up, prev_rhs = blocks_along(package, 1)
    reduced_diag = reduced_diag - prev_diag
    reduced_low = prev_up.T
    reduced_rhs = reduced_rhs - prev_rhs
    level_count = device_count.bit_length() - 1
    zero_block = jnp.zeros_like(identity)
    kept = (identity, zero_block, zero_block, jnp.zeros_like(reduced_rhs))
    odd_flags = []
    for level_index in range(level_count):
        stride = 2**level_index
        active = position % stride == 0
        is_odd = jnp.logical_and(active, position // stride % 2 == 1)
        is_even = jnp.logical_and(active, position // stride % 2 == 0)
        odd_flags.append(is_odd)
        fresh = lax.cond(
            is_odd, eliminate, pass_over, (reduced_diag, reduced_low, reduced_up, reduced_rhs)
        )
        kept = tuple(
            (jnp.where(is_odd, new_part, old_part) for new_part, old_part in zip(fresh, kept))
        )
        factor, w_low, w_up, w_rhs = fresh
        below_terms, above_terms = lax.cond(is_odd, owner_terms, no_terms, (w_low, w_up, w_rhs))
        from_above = blocks_along(below_terms, -stride)
        from_below = blocks_along(above_terms, stride)
        diag_change = from_above[0] + from_below[0]
        reduced_diag = jnp.where(is_even, reduced_diag - diag_change, reduced_diag)
        reduced_up = jnp.where(is_even, from_above[1], reduced_up)
        reduced_low = jnp.where(is_even, from_below[1], reduced_low)
        reduced_rhs = jnp.where(is_even, reduced_rhs - from_above[2] - from_below[2], reduced_rhs)
    solved = lax.cond(position == 0, root_solve, root_skip, (reduced_diag, reduced_rhs))
    for level_index in reversed(range(level_count)):
        stride = 2**level_index
        from_lower = values_along(solved, stride)
        from_upper = values_along(solved, -stride)
        factor, w_low, w_up, w_rhs = kept
        value = upper_solve(
            factor, w_rhs - mproduct(w_low, from_lower) - mproduct(w_up, from_upper)
        )
        solved = jnp.where(odd_flags[level_index], value, solved)
    results = [solved]
    following_sep = values_along(solved, -1)
    next_value = None
    offset = 1
    factor, column_now, link_now = interior[offset - 1]
    spike_now = spikes_full[offset - 1]
    residual_part = (
        column_now
        - mproduct(spike_now[:, :state_width], solved)
        - mproduct(spike_now[:, state_width:], following_sep)
    )
    next_value = upper_solve(factor, residual_part)
    results.insert(1, next_value)
    stacked = jnp.stack(results)
    return jnp.transpose(stacked, (2, 0, 1))


def solution(mesh):
    in_specs = (P("tm", "rhs", None), P("tm", None), P("rhs", "tm", None))
    out_specs = P("rhs", "tm", None)
    return jax.shard_map(
        per_device, mesh=mesh, in_specs=in_specs, out_specs=out_specs, check_vma=False
    )
```

profile of v0, /device:TPU:248, one launch (start us, length us, event | category | flops | bytes accessed | tf_op | source)
XLA Modules:
  0.0 886.1 jit_solution(10605591519088148148)
XLA Ops:
  0.8 13.2 %all_gather.3 = bf16[2,256,256]{2,1,0:T(8,128)(2,1)S(1)} all-gather(bf16[2,32,256]{2,1,0:T(8,128)(2,1)S(1)} %copy-done.53), channel_id=1, replica_groups=mesh['tm'=64,'rhs'=8] {'rhs'}, dimensions={1}, use_global_device_ids=true | all-gather | bytes 294912 | tf_op jit(solution)/shard_map/all_gather | solution.py:98
  15.3 11.7 %cholesky.620 = f32[128,128]{1,0:T(8,128)S(1)} custom-call(f32[128,128]{1,0:T(8,128)S(1)} %cholesky.671), custom_call_target="Cholesky" | custom-call | tf_op jit(solution)/shard_map/jit(cholesky)/cholesky | solution.py:118
  27.0 9.8 %custom-call.80 = f32[1,128,128]{1,2,0:T(8,128)S(1)} custom-call(f32[1,128,128]{2,1,0:T(8,128)S(1)} %get-tuple-element.778), custom_call_target="InvertDiagBlocksLowerTriangular" | custom-call | tf_op jit(solution)/shard_map/jit(cholesky)/cholesky | solution.py:118
  37.3 11.7 %cholesky.637 = f32[128,128]{1,0:T(8,128)S(1)} custom-call(f32[128,128]{1,0:T(8,128)S(1)} %convolution_subtract_fusion.28), custom_call_target="Cholesky" | custom-call | tf_op jit(solution)/shard_map/jit(cholesky)/cholesky | solution.py:118
  51.7 4.1 while.66
  55.8 19.7 %custom-call.20 = f32[2,128,128]{1,2,0:T(8,128)S(1)} custom-call(f32[2,128,128]{2,1,0:T(8,128)S(1)} %get-tuple-element.374), custom_call_target="InvertDiagBlocksLowerTriangular" | custom-call | tf_op jit(solution)/shard_map/triangular_solve | solution.py:16
  79.8 4.7 collective-permute-start
  85.9 3.5 collective-permute-start.2
  89.4 3.5 collective-permute-start.1
  93.0 6.3 collective-permute-done.1
  99.3 63.0 %conditional.13 = (f32[256,256]{1,0:T(8,128)S(1)}, f32[256,256]{1,0:T(8,128)S(1)}, f32[256,256]{1,0:T(8,128)S(1)}, f32[256,8]{0,1:T(8,128)S(1)}) conditional(s32[]{:T(128)} %convert_element_type.84, () %tuple.124, (f32[256,256]{0,1:T(8,128)S(1)}, f32[256,256]{1,0:T(8,128)S(1)}, f32[256,256]{0,1:T(8,128)S(1)}, f32[256,8]{0,1:T(8,128)S(1)}) %tuple.452), branch_computations={%region_5.8_spmd, %region_6.10_spmd} | conditional | flops 357780736 | bytes 7518439 | solution.py:146
  99.7 11.7 %cholesky.382 = f32[128,128]{1,0:T(8,128)S(1)} custom-call(f32[128,128]{1,0:T(8,128)S(1)} %cholesky.653), custom_call_target="Cholesky" | custom-call | tf_op jit(solution)/shard_map/cond/branch_1_fun/jit(cholesky)/cholesky | solution.py:46
  111.4 9.8 %custom-call.53 = f32[1,128,128]{1,2,0:T(8,128)S(1)} custom-call(f32[1,128,128]{2,1,0:T(8,128)S(1)} %get-tuple-element.728), custom_call_target="InvertDiagBlocksLowerTriangular" | custom-call | tf_op jit(solution)/shard_map/cond/branch_1_fun/jit(cholesky)/cholesky | solution.py:46
  121.8 11.7 %cholesky.399 = f32[128,128]{1,0:T(8,128)S(1)} custom-call(f32[128,128]{1,0:T(8,128)S(1)} %convolution_subtract_fusion.5), custom_call_target="Cholesky" | custom-call | tf_op jit(solution)/shard_map/cond/branch_1_fun/jit(cholesky)/cholesky | solution.py:46
  135.5 4.0 while.59
  139.5 19.7 %custom-call.54 = f32[2,128,128]{1,2,0:T(8,128)S(1)} custom-call(f32[2,128,128]{2,1,0:T(8,128)S(1)} %get-tuple-element.525), custom_call_target="InvertDiagBlocksLowerTriangular" | custom-call | tf_op jit(solution)/shard_map/cond/branch_1_fun/triangular_solve/custom-call.0 | solution.py:16
  163.0 3.4 conditional.14
  171.1 7.2 collective-permute-start.8
  178.4 3.9 collective-permute-start.5
  185.2 7.2 collective-permute-start.4
  192.6 2.4 collective-permute-done.3
  197.3 3.2 conditional.15
  206.1 8.1 collective-permute-start.14
  214.3 4.8 collective-permute-start.11
  221.3 4.8 collective-permute-start.9
  228.7 5.1 collective-permute-done.9
  234.8 3.5 conditional.17
  240.7 3.4 collective-permute-start.18
  246.0 9.9 %collective-permute-start.20 = (f32[256,8]{0,1:T(8,128)S(1)}, f32[256,8]{0,1:T(8,128)S(1)}, u32[]{:S(2)}, u32[]{:S(2)}) collective-permute-start(f32[256,8]{0,1:T(8,128)S(1)} %get-tuple-element.311), channel_id=1, source_target_pairs={{0,32},{8,40},{16,48},{24,56},{32,64},{40,72},{48,80},{56,88},{64,... | collective-permute-start | bytes 24584 | tf_op jit(solution)/shard_map/ppermute | solution.py:12
  256.0 6.4 collective-permute-start.17
  262.5 3.4 collective-permute-start.15
  266.7 8.5 collective-permute-start.16
  275.3 13.2 %collective-permute-done.17 = f32[256,256]{1,0:T(8,128)} collective-permute-done((f32[256,256]{1,0:T(8,128)}, f32[256,256]{1,0:T(8,128)}, u32[]{:S(2)}, u32[]{:S(2)}) %collective-permute-start.17) | collective-permute-done | bytes 262176 | tf_op jit(solution)/shard_map/ppermute | solution.py:12
  290.3 7.3 collective-permute-done.16
  298.6 3.9 conditional.19
  309.4 5.1 collective-permute-start.26
  314.6 3.9 collective-permute-start.23
  323.1 5.1 collective-permute-start.22
  329.7 2.7 collective-permute-done.22
  333.4 3.4 conditional.21
  337.6 2.9 conditional.22
  346.0 6.0 collective-permute-start.28
  353.9 6.0 collective-permute-start.32
  362.0 5.4 collective-permute-start.30
  369.9 2.4 collective-permute-done.29
  372.3 3.3 collective-permute-done.30
  375.6 3.4 conditional.23
  383.8 9.9 %collective-permute-start.34 = (f32[256,256]{0,1:T(8,128)}, f32[256,256]{0,1:T(8,128)}, u32[]{:S(2)}, u32[]{:S(2)}) collective-permute-start(f32[256,256]{0,1:T(8,128)} %copy.57), channel_id=1, source_target_pairs={{0,256},{8,264},{16,272},{24,280},{32,288},{40,296},{48,304},{56,3... | collective-permute-start | bytes 786440 | tf_op jit(solution)/shard_map/ppermute | solution.py:12
  394.9 8.4 collective-permute-start.36
  404.1 3.9 while.67
  409.0 5.6 conditional.25
  415.9 19.7 %custom-call.87 = f32[2,128,128]{1,2,0:T(8,128)S(1)} custom-call(f32[2,128,128]{2,1,0:T(8,128)S(1)} %get-tuple-element.551), custom_call_target="InvertDiagBlocksLowerTriangular" | custom-call | tf_op jit(solution)/shard_map/triangular_solve/custom-call.5 | solution.py:20
  435.6 8.4 collective-permute-start.37
  446.3 3.7 collective-permute-start.40
  450.0 5.8 collective-permute-start.39
  458.0 2.5 collective-permute-start.42
  460.5 4.9 collective-permute-start.41
  467.7 4.0 collective-permute-start.44
  471.7 7.9 collective-permute-start.43
  482.0 4.6 collective-permute-start.46
  486.7 5.5 collective-permute-start.45
  494.4 370.9 %collective-permute-start.48 = (f32[256,8]{0,1:T(8,128)S(1)}, f32[256,8]{0,1:T(8,128)S(1)}, u32[]{:S(2)}, u32[]{:S(2)}) collective-permute-start(f32[256,8]{0,1:T(8,128)S(1)} %maximum_select_fusion.4), channel_id=1, source_target_pairs={{8,0},{16,8},{24,16},{32,24},{40,32},{48,40},{56,48},{64,56},{72,6... | collective-permute-start | bytes 24584 | tf_op jit(solution)/shard_map/ppermute | solution.py:12
  865.3 6.5 collective-permute-start.47
  876.3 6.9 collective-permute-done.49
  (364 shorter events, 119.3 us)
Async XLA Ops:
  13.9 61.6 %copy-start.5 = (bf16[2,256,256]{2,1,0:T(8,128)(2,1)}, bf16[2,256,256]{2,1,0:T(8,128)(2,1)S(1)}, u32[]{:S(2)}) copy-start(bf16[2,256,256]{2,1,0:T(8,128)(2,1)S(1)} %all_gather.3) | copy-start | bytes 786436
  55.8 19.8 %copy-start.58 = (s32[2,2]{1,0:T(2,128)}, s32[2,2]{1,0:T(2,128)S(1)}, u32[]{:S(2)}) copy-start(s32[2,2]{1,0:T(2,128)S(1)} %get-tuple-element.1376) | copy-start | bytes 52
  55.8 28.9 %copy-start.8 = (f32[256,256]{1,0:T(8,128)}, f32[256,256]{1,0:T(8,128)S(1)}, u32[]{:S(2)}) copy-start(f32[256,256]{1,0:T(8,128)S(1)} %get-tuple-element.1297) | copy-start | bytes 786436
  75.5 9.4 %copy-start.21 = (f32[2,128,128]{1,2,0:T(8,128)}, f32[2,128,128]{1,2,0:T(8,128)S(1)}, u32[]{:S(2)}) copy-start(f32[2,128,128]{1,2,0:T(8,128)S(1)} %custom-call.20) | copy-start | bytes 393220
  79.8 13.1 %collective-permute-start = (f32[256,256]{0,1:T(8,128)S(1)}, f32[256,256]{0,1:T(8,128)S(1)}, u32[]{:S(2)}, u32[]{:S(2)}) collective-permute-start(f32[256,256]{0,1:T(8,128)S(1)} %get-tuple-element.774), channel_id=1, source_target_pairs={{0,8},{8,16},{16,24},{24,32},{32,40},{40,48},{48,56},{56,64},{64,7... | collective-permute-start | bytes 786440 | tf_op jit(solution)/shard_map/ppermute | solution.py:12
  85.9 7.0 collective-permute-start.2
  89.4 9.9 %collective-permute-start.1 = (f32[256,256]{0,1:T(8,128)S(1)}, f32[256,256]{0,1:T(8,128)S(1)}, u32[]{:S(2)}, u32[]{:S(2)}) collective-permute-start(f32[256,256]{0,1:T(8,128)S(1)} %get-tuple-element.773), channel_id=1, source_target_pairs={{0,8},{8,16},{16,24},{24,32},{32,40},{40,48},{48,56},{56,64},{64,7... | collective-permute-start | bytes 786440 | tf_op jit(solution)/shard_map/ppermute | solution.py:12
  167.2 25.3 %collective-permute-start.6 = (f32[256,256]{0,1:T(8,128)S(1)}, f32[256,256]{0,1:T(8,128)}, u32[]{:S(2)}, u32[]{:S(2)}) collective-permute-start(f32[256,256]{0,1:T(8,128)S(1)} %copy.29), channel_id=1, source_target_pairs={{8,0},{16,8},{24,16},{32,24},{40,32},{48,40},{56,48},{64,56},{72,6... | collective-permute-start | bytes 786440 | tf_op jit(solution)/shard_map/ppermute | solution.py:12
  169.1 16.1 %collective-permute-start.7 = (f32[256,8]{0,1:T(8,128)S(1)}, f32[256,8]{0,1:T(8,128)S(1)}, u32[]{:S(2)}, u32[]{:S(2)}) collective-permute-start(f32[256,8]{0,1:T(8,128)S(1)} %get-tuple-element.292), channel_id=1, source_target_pairs={{8,0},{16,8},{24,16},{32,24},{40,32},{48,40},{56,48},{64,56},{72,6... | collective-permute-start | bytes 24584 | tf_op jit(solution)/shard_map/ppermute | solution.py:12
  171.1 21.4 %collective-permute-start.8 = (f32[256,8]{0,1:T(8,128)S(1)}, f32[256,8]{0,1:T(8,128)S(1)}, u32[]{:S(2)}, u32[]{:S(2)}) collective-permute-start(f32[256,8]{0,1:T(8,128)S(1)} %get-tuple-element.293), channel_id=1, source_target_pairs={{0,8},{8,16},{16,24},{24,32},{32,40},{40,48},{48,56},{56,64},{64,7... | collective-permute-start | bytes 24584 | tf_op jit(solution)/shard_map/ppermute | solution.py:12
  178.4 14.2 %collective-permute-start.5 = (f32[256,256]{1,0:T(8,128)}, f32[256,256]{1,0:T(8,128)}, u32[]{:S(2)}, u32[]{:S(2)}) collective-permute-start(f32[256,256]{1,0:T(8,128)} %copy-done.35), channel_id=1, source_target_pairs={{0,8},{8,16},{16,24},{24,32},{32,40},{40,48},{48,56},{56,64},{64,7... | collective-permute-start | bytes 786440 | tf_op jit(solution)/shard_map/ppermute | solution.py:12
  183.1 11.9 %collective-permute-start.3 = (f32[256,256]{0,1:T(8,128)}, f32[256,256]{0,1:T(8,128)}, u32[]{:S(2)}, u32[]{:S(2)}) collective-permute-start(f32[256,256]{0,1:T(8,128)} %copy.25), channel_id=1, source_target_pairs={{8,0},{16,8},{24,16},{32,24},{40,32},{48,40},{56,48},{64,56},{72,6... | collective-permute-start | bytes 786440 | tf_op jit(solution)/shard_map/ppermute | solution.py:12
  185.2 11.1 %collective-permute-start.4 = (f32[256,256]{0,1:T(8,128)S(1)}, f32[256,256]{0,1:T(8,128)S(1)}, u32[]{:S(2)}, u32[]{:S(2)}) collective-permute-start(f32[256,256]{0,1:T(8,128)S(1)} %copy.26), channel_id=1, source_target_pairs={{0,8},{8,16},{16,24},{24,32},{32,40},{40,48},{48,56},{56,64},{64,7... | collective-permute-start | bytes 786440 | tf_op jit(solution)/shard_map/ppermute | solution.py:12
  202.2 24.0 %collective-permute-start.12 = (f32[256,256]{0,1:T(8,128)S(1)}, f32[256,256]{0,1:T(8,128)}, u32[]{:S(2)}, u32[]{:S(2)}) collective-permute-start(f32[256,256]{0,1:T(8,128)S(1)} %copy.36), channel_id=1, source_target_pairs={{16,0},{24,8},{32,16},{40,24},{48,32},{56,40},{64,48},{72,56},{80,... | collective-permute-start | bytes 786440 | tf_op jit(solution)/shard_map/ppermute | solution.py:12
  204.1 17.2 %collective-permute-start.13 = (f32[256,8]{0,1:T(8,128)S(1)}, f32[256,8]{0,1:T(8,128)S(1)}, u32[]{:S(2)}, u32[]{:S(2)}) collective-permute-start(f32[256,8]{0,1:T(8,128)S(1)} %get-tuple-element.301), channel_id=1, source_target_pairs={{16,0},{24,8},{32,16},{40,24},{48,32},{56,40},{64,48},{72,56},{80,... | collective-permute-start | bytes 24584 | tf_op jit(solution)/shard_map/ppermute | solution.py:12
  206.1 20.1 %collective-permute-start.14 = (f32[256,8]{0,1:T(8,128)S(1)}, f32[256,8]{0,1:T(8,128)S(1)}, u32[]{:S(2)}, u32[]{:S(2)}) collective-permute-start(f32[256,8]{0,1:T(8,128)S(1)} %get-tuple-element.302), channel_id=1, source_target_pairs={{0,16},{8,24},{16,32},{24,40},{32,48},{40,56},{48,64},{56,72},{64,... | collective-permute-start | bytes 24584 | tf_op jit(solution)/shard_map/ppermute | solution.py:12
  214.3 12.0 %collective-permute-start.11 = (f32[256,256]{1,0:T(8,128)}, f32[256,256]{1,0:T(8,128)}, u32[]{:S(2)}, u32[]{:S(2)}) collective-permute-start(f32[256,256]{1,0:T(8,128)} %get-tuple-element.611), channel_id=1, source_target_pairs={{0,16},{8,24},{16,32},{24,40},{32,48},{40,56},{48,64},{56,72},{64,... | collective-permute-start | bytes 786440 | tf_op jit(solution)/shard_map/ppermute | solution.py:12
  219.2 9.5 %collective-permute-start.10 = (f32[256,256]{0,1:T(8,128)S(1)}, f32[256,256]{0,1:T(8,128)}, u32[]{:S(2)}, u32[]{:S(2)}) collective-permute-start(f32[256,256]{0,1:T(8,128)S(1)} %copy.33), channel_id=1, source_target_pairs={{0,16},{8,24},{16,32},{24,40},{32,48},{40,56},{48,64},{56,72},{64,... | collective-permute-start | bytes 786440 | tf_op jit(solution)/shard_map/ppermute | solution.py:12
  221.3 12.5 %collective-permute-start.9 = (f32[256,256]{0,1:T(8,128)S(1)}, f32[256,256]{0,1:T(8,128)S(1)}, u32[]{:S(2)}, u32[]{:S(2)}) collective-permute-start(f32[256,256]{0,1:T(8,128)S(1)} %copy.32), channel_id=1, source_target_pairs={{16,0},{24,8},{32,16},{40,24},{48,32},{56,40},{64,48},{72,56},{80,... | collective-permute-start | bytes 786440 | tf_op jit(solution)/shard_map/ppermute | solution.py:12
  240.7 34.5 %collective-permute-start.18 = (f32[256,256]{0,1:T(8,128)}, f32[256,256]{0,1:T(8,128)}, u32[]{:S(2)}, u32[]{:S(2)}) collective-permute-start(f32[256,256]{0,1:T(8,128)} %copy.43), channel_id=1, source_target_pairs={{32,0},{40,8},{48,16},{56,24},{64,32},{72,40},{80,48},{88,56},{96,... | collective-permute-start | bytes 786440 | tf_op jit(solution)/shard_map/ppermute | solution.py:12
  244.0 22.7 %collective-permute-start.19 = (f32[256,8]{0,1:T(8,128)S(1)}, f32[256,8]{0,1:T(8,128)S(1)}, u32[]{:S(2)}, u32[]{:S(2)}) collective-permute-start(f32[256,8]{0,1:T(8,128)S(1)} %get-tuple-element.310), channel_id=1, source_target_pairs={{32,0},{40,8},{48,16},{56,24},{64,32},{72,40},{80,48},{88,56},{96,... | collective-permute-start | bytes 24584 | tf_op jit(solution)/shard_map/ppermute | solution.py:12
  246.0 29.2 %collective-permute-start.20 = (f32[256,8]{0,1:T(8,128)S(1)}, f32[256,8]{0,1:T(8,128)S(1)}, u32[]{:S(2)}, u32[]{:S(2)}) collective-permute-start(f32[256,8]{0,1:T(8,128)S(1)} %get-tuple-element.311), channel_id=1, source_target_pairs={{0,32},{8,40},{16,48},{24,56},{32,64},{40,72},{48,80},{56,88},{64,... | collective-permute-start | bytes 24584 | tf_op jit(solution)/shard_map/ppermute | solution.py:12
  256.0 32.5 %collective-permute-start.17 = (f32[256,256]{1,0:T(8,128)}, f32[256,256]{1,0:T(8,128)}, u32[]{:S(2)}, u32[]{:S(2)}) collective-permute-start(f32[256,256]{1,0:T(8,128)} %get-tuple-element.612), channel_id=1, source_target_pairs={{0,32},{8,40},{16,48},{24,56},{32,64},{40,72},{48,80},{56,88},{64,... | collective-permute-start | bytes 786440 | tf_op jit(solution)/shard_map/ppermute | solution.py:12
  262.5 27.8 %collective-permute-start.15 = (f32[256,256]{0,1:T(8,128)S(1)}, f32[256,256]{0,1:T(8,128)}, u32[]{:S(2)}, u32[]{:S(2)}) collective-permute-start(f32[256,256]{0,1:T(8,128)S(1)} %copy.39), channel_id=1, source_target_pairs={{32,0},{40,8},{48,16},{56,24},{64,32},{72,40},{80,48},{88,56},{96,... | collective-permute-start | bytes 786440 | tf_op jit(solution)/shard_map/ppermute | solution.py:12
  266.7 30.9 %collective-permute-start.16 = (f32[256,256]{0,1:T(8,128)}, f32[256,256]{0,1:T(8,128)S(1)}, u32[]{:S(2)}, u32[]{:S(2)}) collective-permute-start(f32[256,256]{0,1:T(8,128)} %copy.40), channel_id=1, source_target_pairs={{0,32},{8,40},{16,48},{24,56},{32,64},{40,72},{48,80},{56,88},{64,... | collective-permute-start | bytes 786440 | tf_op jit(solution)/shard_map/ppermute | solution.py:12
  275.3 23.4 %copy-start.19 = (f32[256,256]{0,1:T(8,128)}, f32[256,256]{0,1:T(8,128)S(1)}, u32[]{:S(2)}) copy-start(f32[256,256]{0,1:T(8,128)S(1)} %broadcast_select_fusion.5) | copy-start | bytes 786436
  305.5 23.3 %collective-permute-start.24 = (f32[256,256]{0,1:T(8,128)}, f32[256,256]{0,1:T(8,128)}, u32[]{:S(2)}, u32[]{:S(2)}) collective-permute-start(f32[256,256]{0,1:T(8,128)} %copy.50), channel_id=1, source_target_pairs={{64,0},{72,8},{80,16},{88,24},{96,32},{104,40},{112,48},{120,56},{... | collective-permute-start | bytes 786440 | tf_op jit(solution)/shard_map/ppermute | solution.py:12
  307.4 15.7 %collective-permute-start.25 = (f32[256,8]{0,1:T(8,128)S(1)}, f32[256,8]{0,1:T(8,128)S(1)}, u32[]{:S(2)}, u32[]{:S(2)}) collective-permute-start(f32[256,8]{0,1:T(8,128)S(1)} %get-tuple-element.319), channel_id=1, source_target_pairs={{64,0},{72,8},{80,16},{88,24},{96,32},{104,40},{112,48},{120,56},{... | collective-permute-start | bytes 24584 | tf_op jit(solution)/shard_map/ppermute | solution.py:12
  309.4 18.9 %collective-permute-start.26 = (f32[256,8]{0,1:T(8,128)S(1)}, f32[256,8]{0,1:T(8,128)S(1)}, u32[]{:S(2)}, u32[]{:S(2)}) collective-permute-start(f32[256,8]{0,1:T(8,128)S(1)} %get-tuple-element.320), channel_id=1, source_target_pairs={{0,64},{8,72},{16,80},{24,88},{32,96},{40,104},{48,112},{56,120},{... | collective-permute-start | bytes 24584 | tf_op jit(solution)/shard_map/ppermute | solution.py:12
  314.6 14.3 %collective-permute-start.23 = (f32[256,256]{1,0:T(8,128)}, f32[256,256]{1,0:T(8,128)}, u32[]{:S(2)}, u32[]{:S(2)}) collective-permute-start(f32[256,256]{1,0:T(8,128)} %get-tuple-element.613), channel_id=1, source_target_pairs={{0,64},{8,72},{16,80},{24,88},{32,96},{40,104},{48,112},{56,120},{... | collective-permute-start | bytes 786440 | tf_op jit(solution)/shard_map/ppermute | solution.py:12
  319.3 10.3 %collective-permute-start.21 = (f32[256,256]{0,1:T(8,128)}, f32[256,256]{0,1:T(8,128)}, u32[]{:S(2)}, u32[]{:S(2)}) collective-permute-start(f32[256,256]{0,1:T(8,128)} %copy.46), channel_id=1, source_target_pairs={{64,0},{72,8},{80,16},{88,24},{96,32},{104,40},{112,48},{120,56},{... | collective-permute-start | bytes 786440 | tf_op jit(solution)/shard_map/ppermute | solution.py:12
  321.3 7.6 copy-start.20
  323.1 9.3 %collective-permute-start.22 = (f32[256,256]{0,1:T(8,128)}, f32[256,256]{0,1:T(8,128)S(1)}, u32[]{:S(2)}, u32[]{:S(2)}) collective-permute-start(f32[256,256]{0,1:T(8,128)} %copy.47), channel_id=1, source_target_pairs={{0,64},{8,72},{16,80},{24,88},{32,96},{40,104},{48,112},{56,120},{... | collective-permute-start | bytes 786440 | tf_op jit(solution)/shard_map/ppermute | solution.py:12
  342.3 25.8 %collective-permute-start.27 = (f32[256,256]{0,1:T(8,128)}, f32[256,256]{0,1:T(8,128)}, u32[]{:S(2)}, u32[]{:S(2)}) collective-permute-start(f32[256,256]{0,1:T(8,128)} %copy.52), channel_id=1, source_target_pairs={{128,0},{136,8},{144,16},{152,24},{160,32},{168,40},{176,48},{184,... | collective-permute-start | bytes 786440 | tf_op jit(solution)/shard_map/ppermute | solution.py:12
  346.0 22.1 %collective-permute-start.28 = (f32[256,256]{0,1:T(8,128)}, f32[256,256]{0,1:T(8,128)}, u32[]{:S(2)}, u32[]{:S(2)}) collective-permute-start(f32[256,256]{0,1:T(8,128)} %copy.53), channel_id=1, source_target_pairs={{0,128},{8,136},{16,144},{24,152},{32,160},{40,168},{48,176},{56,1... | collective-permute-start | bytes 786440 | tf_op jit(solution)/shard_map/ppermute | solution.py:12
  352.0 10.0 %collective-permute-start.31 = (f32[256,8]{0,1:T(8,128)S(1)}, f32[256,8]{0,1:T(8,128)S(1)}, u32[]{:S(2)}, u32[]{:S(2)}) collective-permute-start(f32[256,8]{0,1:T(8,128)S(1)} %get-tuple-element.328), channel_id=1, source_target_pairs={{128,0},{136,8},{144,16},{152,24},{160,32},{168,40},{176,48},{184,... | collective-permute-start | bytes 24584 | tf_op jit(solution)/shard_map/ppermute | solution.py:12
  353.9 13.5 %collective-permute-start.32 = (f32[256,8]{0,1:T(8,128)S(1)}, f32[256,8]{0,1:T(8,128)S(1)}, u32[]{:S(2)}, u32[]{:S(2)}) collective-permute-start(f32[256,8]{0,1:T(8,128)S(1)} %get-tuple-element.329), channel_id=1, source_target_pairs={{0,128},{8,136},{16,144},{24,152},{32,160},{40,168},{48,176},{56,1... | collective-permute-start | bytes 24584 | tf_op jit(solution)/shard_map/ppermute | solution.py:12
  360.0 7.5 copy-start.45
  360.0 12.3 %collective-permute-start.29 = (f32[256,256]{1,0:T(8,128)}, f32[256,256]{1,0:T(8,128)}, u32[]{:S(2)}, u32[]{:S(2)}) collective-permute-start(f32[256,256]{1,0:T(8,128)} %get-tuple-element.614), channel_id=1, source_target_pairs={{0,128},{8,136},{16,144},{24,152},{32,160},{40,168},{48,176},{56,1... | collective-permute-start | bytes 786440 | tf_op jit(solution)/shard_map/ppermute | solution.py:12
  362.0 13.6 %collective-permute-start.30 = (f32[256,256]{1,0:T(8,128)}, f32[256,256]{1,0:T(8,128)}, u32[]{:S(2)}, u32[]{:S(2)}) collective-permute-start(f32[256,256]{1,0:T(8,128)} %get-tuple-element.327), channel_id=1, source_target_pairs={{128,0},{136,8},{144,16},{152,24},{160,32},{168,40},{176,48},{184,... | collective-permute-start | bytes 786440 | tf_op jit(solution)/shard_map/ppermute | solution.py:12
  380.8 22.6 %copy-start.29 = (f32[256,256]{1,0:T(8,128)S(1)}, f32[256,256]{1,0:T(8,128)}, u32[]{:S(2)}) copy-start(f32[256,256]{1,0:T(8,128)} %copy-done.28) | copy-start | bytes 786436
  380.8 22.6 %copy-start.32 = (f32[256,256]{1,0:T(8,128)S(1)}, f32[256,256]{1,0:T(8,128)}, u32[]{:S(2)}) copy-start(f32[256,256]{1,0:T(8,128)} %copy-done.31) | copy-start | bytes 786436
  381.6 26.5 %collective-permute-start.33 = (f32[256,256]{0,1:T(8,128)}, f32[256,256]{0,1:T(8,128)}, u32[]{:S(2)}, u32[]{:S(2)}) collective-permute-start(f32[256,256]{0,1:T(8,128)} %copy.56), channel_id=1, source_target_pairs={{256,0},{264,8},{272,16},{280,24},{288,32},{296,40},{304,48},{312,... | collective-permute-start | bytes 786440 | tf_op jit(solution)/shard_map/ppermute | solution.py:12
  382.9 20.5 %copy-start.25 = (f32[256,256]{1,0:T(8,128)S(1)}, f32[256,256]{1,0:T(8,128)}, u32[]{:S(2)}) copy-start(f32[256,256]{1,0:T(8,128)} %copy-done.24) | copy-start | bytes 786436
  382.9 20.5 %copy-start.27 = (f32[256,256]{1,0:T(8,128)S(1)}, f32[256,256]{1,0:T(8,128)}, u32[]{:S(2)}) copy-start(f32[256,256]{1,0:T(8,128)} %copy-done.26) | copy-start | bytes 786436
  383.8 24.4 %collective-permute-start.34 = (f32[256,256]{0,1:T(8,128)}, f32[256,256]{0,1:T(8,128)}, u32[]{:S(2)}, u32[]{:S(2)}) collective-permute-start(f32[256,256]{0,1:T(8,128)} %copy.57), channel_id=1, source_target_pairs={{0,256},{8,264},{16,272},{24,280},{32,288},{40,296},{48,304},{56,3... | collective-permute-start | bytes 786440 | tf_op jit(solution)/shard_map/ppermute | solution.py:12
  393.6 14.5 %collective-permute-start.35 = (f32[256,8]{0,1:T(8,128)S(1)}, f32[256,8]{0,1:T(8,128)S(1)}, u32[]{:S(2)}, u32[]{:S(2)}) collective-permute-start(f32[256,8]{0,1:T(8,128)S(1)} %get-tuple-element.341), channel_id=1, source_target_pairs={{256,0},{264,8},{272,16},{280,24},{288,32},{296,40},{304,48},{312,... | collective-permute-start | bytes 24584 | tf_op jit(solution)/shard_map/ppermute | solution.py:12
  394.9 13.2 %collective-permute-start.36 = (f32[256,8]{0,1:T(8,128)S(1)}, f32[256,8]{0,1:T(8,128)S(1)}, u32[]{:S(2)}, u32[]{:S(2)}) collective-permute-start(f32[256,8]{0,1:T(8,128)S(1)} %get-tuple-element.342), channel_id=1, source_target_pairs={{0,256},{8,264},{16,272},{24,280},{32,288},{40,296},{48,304},{56,3... | collective-permute-start | bytes 24584 | tf_op jit(solution)/shard_map/ppermute | solution.py:12
  408.9 6.9 copy-start.39
  408.9 6.9 copy-start.42
  414.6 29.5 %collective-permute-start.38 = (f32[256,8]{0,1:T(8,128)S(1)}, f32[256,8]{0,1:T(8,128)S(1)}, u32[]{:S(2)}, u32[]{:S(2)}) collective-permute-start(f32[256,8]{0,1:T(8,128)S(1)} %get-tuple-element.1295), channel_id=1, source_target_pairs={{256,0},{264,8},{272,16},{280,24},{288,32},{296,40},{304,48},{312,... | collective-permute-start | bytes 24584 | tf_op jit(solution)/shard_map/ppermute | solution.py:12
  435.6 9.8 %collective-permute-start.37 = (f32[256,8]{0,1:T(8,128)S(1)}, f32[256,8]{0,1:T(8,128)S(1)}, u32[]{:S(2)}, u32[]{:S(2)}) collective-permute-start(f32[256,8]{0,1:T(8,128)S(1)} %get-tuple-element.1295), channel_id=1, source_target_pairs={{0,256},{8,264},{16,272},{24,280},{32,288},{40,296},{48,304},{56,3... | collective-permute-start | bytes 24584 | tf_op jit(solution)/shard_map/ppermute | solution.py:12
  446.3 9.4 %collective-permute-start.40 = (f32[256,8]{0,1:T(8,128)S(1)}, f32[256,8]{0,1:T(8,128)S(1)}, u32[]{:S(2)}, u32[]{:S(2)}) collective-permute-start(f32[256,8]{0,1:T(8,128)S(1)} %maximum_select_fusion), channel_id=1, source_target_pairs={{128,0},{136,8},{144,16},{152,24},{160,32},{168,40},{176,48},{184,... | collective-permute-start | bytes 24584 | tf_op jit(solution)/shard_map/ppermute | solution.py:12
  450.0 7.1 collective-permute-start.39
  458.0 7.5 collective-permute-start.42
  460.5 6.3 collective-permute-start.41
  467.7 11.9 %collective-permute-start.44 = (f32[256,8]{0,1:T(8,128)S(1)}, f32[256,8]{0,1:T(8,128)S(1)}, u32[]{:S(2)}, u32[]{:S(2)}) collective-permute-start(f32[256,8]{0,1:T(8,128)S(1)} %maximum_select_fusion.2), channel_id=1, source_target_pairs={{32,0},{40,8},{48,16},{56,24},{64,32},{72,40},{80,48},{88,56},{96,... | collective-permute-start | bytes 24584 | tf_op jit(solution)/shard_map/ppermute | solution.py:12
  471.7 9.5 %collective-permute-start.43 = (f32[256,8]{0,1:T(8,128)S(1)}, f32[256,8]{0,1:T(8,128)S(1)}, u32[]{:S(2)}, u32[]{:S(2)}) collective-permute-start(f32[256,8]{0,1:T(8,128)S(1)} %maximum_select_fusion.2), channel_id=1, source_target_pairs={{0,32},{8,40},{16,48},{24,56},{32,64},{40,72},{48,80},{56,88},{64,... | collective-permute-start | bytes 24584 | tf_op jit(solution)/shard_map/ppermute | solution.py:12
  482.0 10.1 %collective-permute-start.46 = (f32[256,8]{0,1:T(8,128)S(1)}, f32[256,8]{0,1:T(8,128)S(1)}, u32[]{:S(2)}, u32[]{:S(2)}) collective-permute-start(f32[256,8]{0,1:T(8,128)S(1)} %maximum_select_fusion.3), channel_id=1, source_target_pairs={{16,0},{24,8},{32,16},{40,24},{48,32},{56,40},{64,48},{72,56},{80,... | collective-permute-start | bytes 24584 | tf_op jit(solution)/shard_map/ppermute | solution.py:12
  486.7 6.8 collective-permute-start.45
  494.4 377.4 %collective-permute-start.48 = (f32[256,8]{0,1:T(8,128)S(1)}, f32[256,8]{0,1:T(8,128)S(1)}, u32[]{:S(2)}, u32[]{:S(2)}) collective-permute-start(f32[256,8]{0,1:T(8,128)S(1)} %maximum_select_fusion.4), channel_id=1, source_target_pairs={{8,0},{16,8},{24,16},{32,24},{40,32},{48,40},{56,48},{64,56},{72,6... | collective-permute-start | bytes 24584 | tf_op jit(solution)/shard_map/ppermute | solution.py:12
  865.3 7.8 collective-permute-start.47
  874.1 9.1 %collective-permute-start.49 = (f32[256,8]{0,1:T(8,128)S(1)}, f32[256,8]{0,1:T(8,128)S(1)}, u32[]{:S(2)}, u32[]{:S(2)}) collective-permute-start(f32[256,8]{0,1:T(8,128)S(1)} %maximum_select_fusion.5), channel_id=1, source_target_pairs={{8,0},{16,8},{24,16},{32,24},{40,32},{48,40},{56,48},{64,56},{72,6... | collective-permute-start | bytes 24584 | tf_op jit(solution)/shard_map/ppermute | solution.py:12
  876.3 7.2 copy-start.22
  (27 other events, 45.4 us)
where the time goes:
time: 897 us; the launch traced here: 886 us
  starting transfers between devices  585 us (65%)
  other arithmetic  139 us (15%)
  waiting for transfers between devices  61.8 us (7%)
  local copies, waits for them, and re-layouts  41.3 us (5%)
  loops' own time  24.2 us (3%)
  matrix products  18.2 us (2%)
  blocking collectives  13.2 us (1%)
    ppermute x50, starting transfers between devices, passed_along(): return lax.ppermute(value, axis, pairs)  585 us
    ppermute x50, waiting for transfers between devices, passed_along(): return lax.ppermute(value, axis, pairs)  61.8 us
    another operation x10, other arithmetic, lower_solve(): lax.linalg.triangular_solve(factor, values, left_side=True, lower=True)  39.5 us
    another operation x7, other arithmetic, per_device(): factor = jnp.linalg.cholesky(hess_block)  34.6 us
    another operation x6, other arithmetic, eliminate(): factor = jnp.linalg.cholesky(reduced_diag)  34 us
    another operation x2, other arithmetic, upper_solve(): lax.linalg.triangular_solve(factor, values, left_side=True, lower=True, t...  19.8 us
  transfers between devices with their start and end apart: 50, of which 18 were waited for; matrix products, arithmetic and copies ran while one was open for 4% of the time, Pallas kernels for 0%

commit v1 on v0

v1 whole, which is shorter than its diff:
```python
import functools

import jax
import jax.numpy as jnp
from jax import lax
from jax.experimental import pallas as pl
from jax.experimental.pallas import tpu as pltpu
from jax.sharding import PartitionSpec as P

HIGHEST = lax.Precision.HIGHEST
F32 = jnp.float32
N = 256
H = 128


def nn(a, b):
    return lax.dot_general(a, b, (((1,), (0,)), ((), ())), precision=HIGHEST, preferred_element_type=F32)


def nt(a, b):
    return lax.dot_general(a, b, (((1,), (1,)), ((), ())), precision=HIGHEST, preferred_element_type=F32)


def spread(x):
    return jnp.broadcast_to(x, (8, 128))


def inverse_of(x):
    guess = pl.reciprocal(x, approx=True)
    return guess + guess * (1.0 - x * guess)


def sweep8(entries):
    get = lambda i, j: entries[(min(i, j), max(i, j))]
    for a in range(0, 8, 2):
        b = a + 1
        aa, ab, bb = get(a, a), get(a, b), get(b, b)
        scale = inverse_of(aa * bb - ab * ab)
        others = [i for i in range(8) if i not in (a, b)]
        part = {i: (bb * get(i, a) - ab * get(i, b), aa * get(i, b) - ab * get(i, a)) for i in others}
        new = {}
        for place, i in enumerate(others):
            for j in others[place:]:
                new[(i, j)] = get(i, j) - (part[i][0] * get(j, a) + part[i][1] * get(j, b)) * scale
        for i in others:
            new[(min(i, a), max(i, a))] = part[i][0] * scale
            new[(min(i, b), max(i, b))] = part[i][1] * scale
        new[(a, a)], new[(b, b)], new[(a, b)] = -bb * scale, -aa * scale, ab * scale
        entries = new
    return entries


def tree_sum(terms):
    while len(terms) > 1:
        terms = [terms[i] + terms[i + 1] for i in range(0, len(terms), 2)]
    return terms[0]


def sweep(ref):
    lane = lax.broadcasted_iota(jnp.int32, (8, 128), 1)
    sub = lax.broadcasted_iota(jnp.int32, (8, 128), 0)
    rows = [ref[8 * g : 8 * g + 8, :] for g in range(16)]
    for w in range(16):
        k0 = 8 * w
        pivots = rows[w]
        cols = [spread(pivots[:, k0 + j : k0 + j + 1]) for j in range(8)]
        entries = {(i, j): spread(cols[j][i : i + 1, :]) for j in range(8) for i in range(j + 1)}
        inside = (lane >= k0) & (lane < k0 + 8)
        panel = []
        for j in range(8):
            row = spread(pivots[j : j + 1, :])
            panel.append(jnp.where(inside, jnp.where(lane == k0 + j, -1.0, 0.0), row))
        swept = sweep8(entries)
        minus = [tree_sum([swept[(min(i, j), max(i, j))] * panel[j] for j in range(8)]) for i in range(8)]
        for g in list(range(w + 1, 16)) + list(range(w)):
            terms = [spread(rows[g][:, k0 + j : k0 + j + 1]) * minus[j] for j in range(8)]
            rows[g] = jnp.where(inside, 0.0, rows[g]) + tree_sum(terms)
        new = minus[7]
        for i in range(6, -1, -1):
            new = jnp.where(sub == i, minus[i], new)
        rows[w] = -new
    for g in range(16):
        ref[8 * g : 8 * g + 8, :] = rows[g]


def kernel(
    width, peers, levels,
    jac, damp, rhs, out,
    whole, diag, links, half, gain, t_out, r_out, c_out, t_in, r_in, x_own, x_in,
    j_send, j_recv, m_send, t_recv, a_recv, x_send, x_recv,
):
    pos = lax.axis_index("tm")
    me = lax.axis_index("rhs")

    def is_multiple(step):
        return pos % step == 0

    barrier = pltpu.get_barrier_semaphore()
    count = peers - 1
    for d in range(1, peers):
        pl.semaphore_signal(barrier, inc=1, device_id={"rhs": (me + d) % peers}, device_id_type=pl.DeviceIdType.MESH)
    for level in range(levels):
        step = 2**level
        for sign in (-1, 1):
            there = pos + sign * step
            partner = is_multiple(step) & (there >= 0) & (there < width)
            count = count + partner.astype(jnp.int32)

            @pl.when(partner)
            def _(there=there):
                pl.semaphore_signal(barrier, inc=1, device_id={"tm": there}, device_id_type=pl.DeviceIdType.MESH)
    pl.semaphore_wait(barrier, count)

    depth = jac.shape[1]
    mine = pl.ds(pl.multiple_of(me * depth, depth), depth)

    def row_copy(d):
        return pltpu.make_async_remote_copy(
            src_ref=jac, dst_ref=whole.at[:, mine, :], send_sem=j_send.at[d - 1], recv_sem=j_recv.at[d - 1],
            device_id={"rhs": (me + d) % peers}, device_id_type=pl.DeviceIdType.MESH,
        )

    for d in range(1, peers):
        row_copy(d).start()
    whole[:, mine, :] = jac[...]
    for d in range(1, peers):
        row_copy(d).wait()

    on_diag = lax.broadcasted_iota(jnp.int32, (N, N), 0) == lax.broadcasted_iota(jnp.int32, (N, N), 1)
    first = jnp.where(pos > 0, 1.0, 0.0).astype(F32)
    for k in range(2):
        block = lax.dot_general(whole[k], whole[k], (((0,), (0,)), ((), ())), preferred_element_type=F32)
        extra = damp[k : k + 1, :] + (first if k == 0 else 1.0)
        block = block + jnp.where(on_diag, jnp.broadcast_to(extra, (N, N)), 0.0)
        diag[k, 0] = block[:H, :H]
        diag[k, 1] = block[H:, :H]
        diag[k, 2] = block[H:, H:]
    last = jnp.where(pos < width - 1, 1.0, 0.0).astype(F32)
    links[1, 0:N, :] = -whole[0].astype(F32).T
    links[1, N : 2 * N, :] = -whole[1].astype(F32) * last
    for k in range(2):
        links[k, 2 * N : 2 * N + 8, :] = rhs[:, k, :]

    def message(t, blk, side, place, hop, part):
        slot = 1 - side
        if part < 3:
            src, dst, sem = t_out.at[blk, side, part], t_in.at[t, slot, part], t_recv.at[t, slot, part]
        elif part == 3:
            src, dst, sem = r_out.at[blk, side], r_in.at[t, slot], t_recv.at[t, slot, 3]
        else:
            dst = links.at[0, pl.ds(pl.multiple_of(slot * N, N), N), :]
            src, sem = c_out.at[blk], a_recv.at[slot]
        return pltpu.make_async_remote_copy(
            src_ref=src, dst_ref=dst, send_sem=m_send.at[blk, place, part], recv_sem=sem,
            device_id={"tm": pos + hop * (2 * side - 1)}, device_id_type=pl.DeviceIdType.MESH,
        )

    def exists(there):
        return (there >= 0) & (there < width)

    def next_odd_side(t, step):
        quarter = jnp.where(t == 0, 2 * pos + 1, pos // step) % 4
        return jnp.where(quarter == 1, 1, 0)

    def absorb(t, part):
        def take(slot):
            arrival = message(t - 1, 0, 1 - slot, 0, 1, part)
            arrival.wait_recv()
            if part < 3:
                diag[0, part] = diag[0, part] - t_in[t - 1, slot, part]
            else:
                links[0, 2 * N : 2 * N + 8, :] = links[0, 2 * N : 2 * N + 8, :] - r_in[t - 1, slot]

        @pl.when(pos > 0)
        def _():
            take(0)

        @pl.when(t >= 2)
        def _():
            take(1)

    def products(t, blk, step):
        side_o = next_odd_side(t, step)
        hop = jnp.where(t == 0, 1, step)
        for place in range(2):
            side = side_o if place == 0 else 1 - side_o
            rows_at = pl.multiple_of(side * N, N)
            there = pos + hop * (2 * side - 1)
            local = (t == 0) & (side == 0)
            remote = exists(there) & jnp.logical_not(local)

            for part, (r, c) in enumerate(((0, 0), (1, 0), (1, 1))):
                left = gain[blk, pl.ds(rows_at + r * H, H), :]
                right = links[blk, pl.ds(rows_at + c * H, H), :]
                t_out[blk, side, part] = nt(left, right)

                @pl.when(remote)
                def _(part=part, side=side, place=place):
                    message(t, blk, side, place, hop, part).start()
            mat = links[blk, pl.ds(rows_at, N), :]
            r_out[blk, side] = nt(gain[blk, 2 * N : 2 * N + 8, :], mat)

            @pl.when(remote)
            def _(side=side, place=place):
                message(t, blk, side, place, hop, 3).start()

            if place == 0:
                other_at = pl.multiple_of((1 - side) * N, N)
                c_out[blk] = -nt(gain[blk, pl.ds(other_at, N), :], mat)

                @pl.when(remote)
                def _(side=side):
                    message(t, blk, side, 0, hop, 4).start()

            @pl.when(local)
            def _(place=place, side=side):
                for part in range(3):
                    diag[0, part] = diag[0, part] - t_out[blk, side, part]
                links[0, 2 * N : 2 * N + 8, :] = links[0, 2 * N : 2 * N + 8, :] - r_out[blk, side]
                if place == 0:
                    links[0, N : 2 * N, :] = c_out[blk]

    def wait_sent(t, blk, step):
        side_o = next_odd_side(t, step)
        hop = jnp.where(t == 0, 1, step)
        for place in range(2):
            side = side_o if place == 0 else 1 - side_o
            there = pos + hop * (2 * side - 1)
            remote = exists(there) & jnp.logical_not((t == 0) & (side == 0))

            @pl.when(remote)
            def _(side=side, place=place):
                for part in range(5 - place):
                    message(t, blk, side, place, hop, part).wait_send()

    def eliminate(t, step):
        blk = jnp.where(t == 0, 1, 0)
        active = (t >= 1) & (pos % step == 0)
        odd = (t <= levels) & active & (pos // step % 2 == 1)
        root = (t == levels + 1) & (pos == 0)
        invert = (t == 0) | odd | root

        def part_of(h, carry):
            @pl.when(active & (h == 0))
            def _():
                absorb(t, 0)

            @pl.when(active & (h == 1))
            def _():
                for part in (1, 2, 3):
                    absorb(t, part)

            @pl.when(invert & (h == 1))
            def _():
                half[...] = -nn(diag[blk, 1], diag[blk, 0])
                diag[blk, 2] = diag[blk, 2] - nt(half[...], diag[blk, 1])

            @pl.when(invert)
            def _():
                sweep(diag.at[blk, 2 * h])

            return carry

        lax.fori_loop(0, 2, part_of, 0)

        def gains(start, size):
            low = links[blk, start : start + size, :H]
            rest = links[blk, start : start + size, H:] - nt(low, half[...])
            upper = -nn(rest, diag[blk, 2])
            gain[blk, start : start + size, H:] = upper
            gain[blk, start : start + size, :H] = -nn(low, diag[blk, 0]) - nn(upper, half[...])

        @pl.when(odd)
        def _():
            message(t - 1, 0, 1, 0, 1, 4).wait_recv()

            @pl.when(t >= 2)
            def _():
                message(t - 1, 0, 0, 0, 1, 4).wait_recv()

        @pl.when(odd | (t == 0))
        def _():
            gains(0, 2 * N + 8)
            products(t, blk, step)

        @pl.when(odd)
        def _():
            wait_sent(t, blk, step)

        @pl.when(root)
        def _():
            gains(2 * N, 8)

        return jnp.where(t == 0, 1, 2 * step)

    lax.fori_loop(0, levels + 2, eliminate, jnp.int32(1))

    def x_copy(there, slot, index):
        return pltpu.make_async_remote_copy(
            src_ref=x_own, dst_ref=x_in.at[slot], send_sem=x_send.at[index], recv_sem=x_recv.at[slot],
            device_id={"tm": there}, device_id_type=pl.DeviceIdType.MESH,
        )

    def x_targets(level):
        targets = []
        for lower in reversed(range(level)):
            step = 2**lower
            targets.append((pos + step, 0, 2 * lower))
            if lower > 0:
                targets.append((pos - step, 1, 2 * lower + 1))
        targets.append((pos - 1, 2, 1))
        return targets

    def start_x(level):
        for there, slot, index in x_targets(level):
            @pl.when(exists(there))
            def _(there=there, slot=slot, index=index):
                x_copy(there, slot, index).start()

    def wait_x(level):
        for there, slot, index in x_targets(level):
            @pl.when(exists(there))
            def _(there=there, slot=slot, index=index):
                x_copy(there, slot, index).wait_send()

    @pl.when(pos == 0)
    def _():
        x_own[...] = gain[0, 2 * N : 2 * N + 8, :]
        start_x(levels)

    for level in reversed(range(levels)):
        step = 2**level

        @pl.when(pos % (2 * step) == step)
        def _(level=level, step=step):
            side_o = next_odd_side(1, step)
            x_own[...] = gain[0, 2 * N : 2 * N + 8, :]
            for side in (1 - side_o, side_o):
                @pl.when((side == 0) | (pos + step < width))
                def _(side=side):
                    slot = side * (2 if level == 0 else 1)
                    x_copy(pos, slot, 0).wait_recv()
                    x_own[...] = x_own[...] - nn(x_in[slot], gain[0, pl.ds(pl.multiple_of(side * N, N), N), :])
            start_x(level)

    out[:, 0, :] = x_own[...]
    out[:, 1, :] = gain[1, 2 * N : 2 * N + 8, :] - nn(x_own[...], gain[1, 0:N, :])

    @pl.when(pos < width - 1)
    def _():
        @pl.when(pos % 2 == 0)
        def _():
            x_copy(pos, 2, 0).wait_recv()

        out[:, 1, :] = out[:, 1, :] - nn(x_in[2], gain[1, N : 2 * N, :])

    wait_sent(jnp.int32(0), 1, jnp.int32(1))

    @pl.when(pos == 0)
    def _():
        wait_x(levels)

    for level in range(levels):
        @pl.when(pos % (2 * 2**level) == 2**level)
        def _(level=level):
            wait_x(level)


def per_device(jacobians, damping, right_sides):
    width = lax.axis_size("tm")
    peers = lax.axis_size("rhs")
    levels = width.bit_length() - 1
    vmem = pl.BlockSpec(memory_space=pltpu.VMEM)
    return pl.pallas_call(
        functools.partial(kernel, width, peers, levels),
        out_shape=jax.ShapeDtypeStruct(right_sides.shape, F32),
        in_specs=[vmem] * 3,
        out_specs=vmem,
        scratch_shapes=[
            pltpu.VMEM((2, N, N), jnp.bfloat16),
            pltpu.VMEM((2, 3, H, H), F32),
            pltpu.VMEM((2, 2 * N + 8, N), F32),
            pltpu.VMEM((H, H), F32),
            pltpu.VMEM((2, 2 * N + 8, N), F32),
            pltpu.VMEM((2, 2, 3, H, H), F32),
            pltpu.VMEM((2, 2, 8, N), F32),
            pltpu.VMEM((2, N, N), F32),
            pltpu.VMEM((levels + 1, 2, 3, H, H), F32),
            pltpu.VMEM((levels + 1, 2, 8, N), F32),
            pltpu.VMEM((8, N), F32),
            pltpu.VMEM((3, 8, N), F32),
            pltpu.SemaphoreType.DMA((peers - 1,)),
            pltpu.SemaphoreType.DMA((peers - 1,)),
            pltpu.SemaphoreType.DMA((2, 2, 5)),
            pltpu.SemaphoreType.DMA((levels + 1, 2, 4)),
            pltpu.SemaphoreType.DMA((2,)),
            pltpu.SemaphoreType.DMA((2 * levels,)),
            pltpu.SemaphoreType.DMA((3,)),
        ],
        compiler_params=pltpu.CompilerParams(
            collective_id=0, has_side_effects=True, vmem_limit_bytes=32 * 1024 * 1024
        ),
    )(jacobians, damping, right_sides)


def solution(mesh):
    in_specs = (P("tm", "rhs", None), P("tm", None), P("rhs", "tm", None))
    return jax.shard_map(
        per_device, mesh=mesh, in_specs=in_specs, out_specs=P("rhs", "tm", None), check_vma=False
    )
```

time: 897 us -> 178 us (0.20)
  the two profiles are of different devices: /device:TPU:248 before, /device:TPU:16 now
where the time goes in v1:
time: 178 us
  Pallas kernels  175 us (98%)
  local copies, waits for them, and re-layouts  2.76 us (2%)
    pallas_call x1, Pallas kernels, per_device(): pl.pallas_call(functools.partial(kernel, width, peers, levels), out_shape...  175 us

profile of v1, /device:TPU:16, one launch (start us, length us, event | category | flops | bytes accessed | tf_op | source)
XLA Modules:
  0.0 177.6 jit_solution(12384958802682750556)
XLA Ops:
  0.0 0.0 copy-start
  0.0 0.8 copy-done
  0.8 0.0 copy-start.1
  0.8 0.7 copy-done.1
  1.5 0.0 copy-start.2
  1.5 0.7 copy-done.2
  2.2 174.8 %shard_map.37 = f32[8,2,256]{2,1,0:T(2,128)S(1)} custom-call(bf16[2,32,256]{2,1,0:T(8,128)(2,1)S(1)} %copy-done, f32[2,256]{1,0:T(2,128)S(1)} %copy-done.2, f32[8,2,256]{2,1,0:T(2,128)S(1)} %copy-done.1), custom_call_target="tpu_custom_call" | custom-call | tf_op jit(solution)/shard_map/pallas_call | solution.py:374
  176.9 0.6 copy.5
Async XLA Ops:
  0.0 0.8 copy-start
  0.8 0.7 copy-start.1
  1.5 0.7 copy-start.2

commit v2 on v1

v2 whole, which is shorter than its diff:
```python
import functools

import jax
import jax.numpy as jnp
from jax import lax
from jax.experimental import pallas as pl
from jax.experimental.pallas import tpu as pltpu
from jax.sharding import PartitionSpec as P

HIGHEST = lax.Precision.HIGHEST
F32 = jnp.float32
N = 256
H = 128


def nn(a, b):
    return lax.dot_general(a, b, (((1,), (0,)), ((), ())), precision=HIGHEST, preferred_element_type=F32)


def nt(a, b):
    return lax.dot_general(a, b, (((1,), (1,)), ((), ())), precision=HIGHEST, preferred_element_type=F32)


def spread(x):
    return jnp.broadcast_to(x, (8, 128))


def tree_sum(terms):
    while len(terms) > 1:
        terms = [terms[i] + terms[i + 1] for i in range(0, len(terms), 2)]
    return terms[0]


def sweep8(cols, sub):
    for a in range(0, 8, 2):
        b = a + 1
        row_a = [spread(c[a : a + 1, :]) for c in cols]
        row_b = [spread(c[b : b + 1, :]) for c in cols]
        aa, ab, bb = row_a[a], row_a[b], row_b[b]
        det = aa * bb - ab * ab
        guess = pl.reciprocal(det, approx=True)
        mend = 2.0 - det * guess
        is_a, is_b = sub == a, sub == b
        part_a = jnp.where(is_a, -bb, jnp.where(is_b, ab, bb * cols[a] - ab * cols[b])) * guess
        part_b = jnp.where(is_a, ab, jnp.where(is_b, -aa, aa * cols[b] - ab * cols[a])) * guess
        new = []
        for j in range(8):
            if j == a:
                new.append(part_a * mend)
            elif j == b:
                new.append(part_b * mend)
            else:
                kept = jnp.where(is_a | is_b, 0.0, cols[j])
                new.append(kept - (part_a * row_a[j] + part_b * row_b[j]) * mend)
        cols = new
    return cols


def sweep(ref):
    lane = lax.broadcasted_iota(jnp.int32, (8, 128), 1)
    sub = lax.broadcasted_iota(jnp.int32, (8, 128), 0)
    rows = [ref[8 * g : 8 * g + 8, :] for g in range(16)]
    for start in (0, 8):
        panel = range(start, start + 8)
        for w in panel:
            k0 = 8 * w
            inside = (lane >= k0) & (lane < k0 + 8)
            pivots = rows[w]
            cols = sweep8([spread(pivots[:, k0 + j : k0 + j + 1]) + 0.0 for j in range(8)], sub)
            terms = []
            for j in range(8):
                row = jnp.where(inside, jnp.where(lane == k0 + j, -1.0, 0.0), spread(pivots[j : j + 1, :]))
                terms.append(cols[j] * row)
            swept = tree_sum(terms)
            minus = [spread(swept[j : j + 1, :]) for j in range(8)]
            for g in list(range(w + 1, start + 8)) + list(range(start, w)):
                terms = [spread(rows[g][:, k0 + j : k0 + j + 1]) * minus[j] for j in range(8)]
                rows[g] = jnp.where(inside, 0.0, rows[g]) + tree_sum(terms)
            rows[w] = -swept
        others = range(8 - start, 16 - start)
        zero = jnp.zeros((8, 128), F32)
        far = jnp.concatenate([rows[g] for g in others], axis=0)
        near = jnp.concatenate([rows[g] if g in panel else zero for g in range(16)], axis=0)
        change = nn(far, near)
        inside = (lane >= 8 * start) & (lane < 8 * start + 64)
        for index, g in enumerate(others):
            rows[g] = jnp.where(inside, 0.0, rows[g]) - change[8 * index : 8 * index + 8, :]
    for g in range(16):
        ref[8 * g : 8 * g + 8, :] = rows[g]


def kernel(
    width, peers, levels,
    jac, damp, rhs, out,
    whole, damp_in, rhs_in, diag, links, half, full, gain, t_out, r_out, c_out, t_in, r_in,
    d_in, d_rhs, x_root, x_own, x_in,
    i_sem, j_send, j_recv, m_send, t_recv, a_recv, p_send, p_recv, d_send, d_recv, z_send, x_send, x_recv,
):
    pos = lax.axis_index("tm")
    me = lax.axis_index("rhs")
    middle = width // 2
    core = me % 2

    def is_multiple(step):
        return pos % step == 0

    depth = jac.shape[1]
    mine = pl.ds(pl.multiple_of(me * depth, depth), depth)
    loads = [
        pltpu.make_async_copy(jac, whole.at[:, mine, :], i_sem.at[0]),
        pltpu.make_async_copy(damp, damp_in, i_sem.at[1]),
        pltpu.make_async_copy(rhs, rhs_in, i_sem.at[2]),
    ]
    for load in loads:
        load.start()

    barrier = pltpu.get_barrier_semaphore()
    count = peers - 1
    for d in range(1, peers):
        pl.semaphore_signal(barrier, inc=1, device_id={"rhs": (me + d) % peers}, device_id_type=pl.DeviceIdType.MESH)
    partners = [((pos + sign * 2**k), is_multiple(2**k)) for k in range(levels) for sign in (-1, 1)]
    for k in range(levels - 2):
        partners.append((jnp.int32(2**k), pos == middle))
        partners.append((jnp.int32(middle), pos == 2**k))
    for there, holds in partners:
        partner = holds & (there >= 0) & (there < width)
        count = count + partner.astype(jnp.int32)

        @pl.when(partner)
        def _(there=there):
            pl.semaphore_signal(barrier, inc=1, device_id={"tm": there}, device_id_type=pl.DeviceIdType.MESH)
    pl.semaphore_wait(barrier, count)

    def row_copy(d):
        return pltpu.make_async_remote_copy(
            src_ref=jac, dst_ref=whole.at[:, mine, :], send_sem=j_send.at[d - 1], recv_sem=j_recv.at[d - 1],
            device_id={"rhs": (me + d) % peers}, device_id_type=pl.DeviceIdType.MESH,
        )

    for d in range(1, peers):
        row_copy(d).start()
    for load in loads:
        load.wait()
    for d in range(1, peers):
        row_copy(d).wait()

    on_diag = lax.broadcasted_iota(jnp.int32, (N, N), 0) == lax.broadcasted_iota(jnp.int32, (N, N), 1)
    first = jnp.where(pos > 0, 1.0, 0.0).astype(F32)
    for k in range(2):
        block = lax.dot_general(whole[k], whole[k], (((0,), (0,)), ((), ())), preferred_element_type=F32)
        extra = damp_in[k : k + 1, :] + (first if k == 0 else 1.0)
        block = block + jnp.where(on_diag, jnp.broadcast_to(extra, (N, N)), 0.0)
        diag[k, 0] = block[:H, :H]
        diag[k, 1] = block[H:, :H]
        diag[k, 2] = block[H:, H:]
    last = jnp.where(pos < width - 1, 1.0, 0.0).astype(F32)
    links[1, 0:N, :] = -whole[0].astype(F32).T
    links[1, N : 2 * N, :] = -whole[1].astype(F32) * last
    for k in range(2):
        links[k, 2 * N : 2 * N + 8, :] = rhs_in[:, k, :]

    def coupling_half(slot, which):
        return links.at[0, pl.ds(pl.multiple_of(slot * N + which * H, H), H), :]

    def pair_copy(slot):
        return pltpu.make_async_remote_copy(
            src_ref=coupling_half(slot, core), dst_ref=coupling_half(slot, core), send_sem=p_send.at[slot],
            recv_sem=p_recv.at[slot], device_id={"rhs": me + 1 - 2 * core}, device_id_type=pl.DeviceIdType.MESH,
        )

    def root_copy(part):
        if part < 3:
            src, dst = diag.at[0, part], d_in.at[part]
        else:
            src, dst = links.at[0, 2 * N : 2 * N + 8, :], d_rhs
        return pltpu.make_async_remote_copy(
            src_ref=src, dst_ref=dst, send_sem=d_send.at[part], recv_sem=d_recv.at[part],
            device_id={"tm": middle}, device_id_type=pl.DeviceIdType.MESH,
        )

    def message(t, blk, side, place, hop, part):
        slot = 1 - side
        if part < 3:
            src, dst, sem = t_out.at[blk, side, part], t_in.at[t, slot, part], t_recv.at[t, slot, part]
        elif part == 3:
            src, dst, sem = r_out.at[blk, side], r_in.at[t, slot], t_recv.at[t, slot, 3]
        else:
            dst = coupling_half(slot, core)
            src, sem = c_out.at[blk], a_recv.at[slot]
        return pltpu.make_async_remote_copy(
            src_ref=src, dst_ref=dst, send_sem=m_send.at[blk, place, part], recv_sem=sem,
            device_id={"tm": pos + hop * (2 * side - 1)}, device_id_type=pl.DeviceIdType.MESH,
        )

    def exists(there):
        return (there >= 0) & (there < width)

    def next_odd_side(t, step):
        quarter = jnp.where(t == 0, 2 * pos + 1, pos // step) % 4
        return jnp.where(quarter == 1, 1, 0)

    def absorb(t, part):
        def take(slot):
            arrival = message(t - 1, 0, 1 - slot, 0, 1, part)
            arrival.wait_recv()
            if part < 3:
                diag[0, part] = diag[0, part] - t_in[t - 1, slot, part]
            else:
                links[0, 2 * N : 2 * N + 8, :] = links[0, 2 * N : 2 * N + 8, :] - r_in[t - 1, slot]

        @pl.when(pos > 0)
        def _():
            take(0)

        @pl.when(t >= 2)
        def _():
            take(1)

    def products(t, blk, step):
        side_o = next_odd_side(t, step)
        hop = jnp.where(t == 0, 1, step)
        last = t == levels
        y_rows = slice(2 * N, 2 * N + 8)

        def gains(start, size):
            rows = pl.ds(start, size)
            gain[blk, rows, :] = nn(links[blk, rows, :], full[...])

        for place in range(2):
            side = side_o if place == 0 else 1 - side_o
            at = pl.multiple_of(side * N, N)
            other_at = pl.multiple_of((1 - side) * N, N)
            there = pos + hop * (2 * side - 1)
            local = (t == 0) & (side == 0)
            remote = exists(there) & jnp.logical_not(local | last)

            def send(part):
                @pl.when(remote)
                def _():
                    message(t, blk, side, place, hop, part).start()

            def give():
                for part, (r, c) in enumerate(((0, 0), (1, 0), (1, 1))):
                    left = pl.ds(pl.multiple_of(at + r * H, H), H)
                    right = pl.ds(pl.multiple_of(at + c * H, H), H)
                    if part < 2:
                        gains(pl.multiple_of(at + r * H, H), H)
                    t_out[blk, side, part] = nt(gain[blk, left, :], links[blk, right, :])
                    send(part)
                if place == 0:
                    gains(2 * N, 8)
                mat = links[blk, pl.ds(at, N), :]
                r_out[blk, side] = nt(gain[blk, y_rows, :], mat)
                send(3)

                if place == 0:
                    own = pl.ds(pl.multiple_of(other_at + core * H, H), H)
                    gains(pl.multiple_of(other_at + core * H, H), H)
                    c_out[blk] = -nt(gain[blk, own, :], mat)
                    send(4)

                @pl.when(local)
                def _():
                    for part in range(3):
                        diag[0, part] = diag[0, part] - t_out[blk, side, part]
                    links[0, y_rows, :] = links[0, y_rows, :] - r_out[blk, side]
                    if place == 0:
                        gains(other_at, N)
                        links[0, N : 2 * N, :] = -nt(gain[blk, pl.ds(other_at, N), :], mat)

            if place == 0:
                pl.when(jnp.logical_not(last))(give)

                @pl.when(last)
                def _():
                    gains(2 * N, 8)
            else:
                give()

        @pl.when(last)
        def _():
            for part in range(4):
                root_copy(part).wait_recv()
            for part in range(3):
                diag[0, part] = d_in[part] - t_out[blk, 0, part]
            d_rhs[...] = d_rhs[...] - r_out[blk, 0]

    def wait_sent(t, blk, step):
        side_o = next_odd_side(t, step)
        hop = jnp.where(t == 0, 1, step)
        for place in range(2):
            side = side_o if place == 0 else 1 - side_o
            there = pos + hop * (2 * side - 1)
            remote = exists(there) & jnp.logical_not(((t == 0) & (side == 0)) | (t == levels))

            @pl.when(remote)
            def _(side=side, place=place):
                for part in range(5 - place):
                    message(t, blk, side, place, hop, part).wait_send()

    def eliminate(t, step):
        blk = jnp.where(t == 0, 1, 0)
        active = (t >= 1) & (t <= levels) & (pos % step == 0)
        odd = active & (pos // step % 2 == 1)
        root = (t == levels + 1) & (pos == middle)
        invert = (t == 0) | odd | root

        def part_of(h, carry):
            @pl.when(active & (h == 0))
            def _():
                absorb(t, 0)

            @pl.when(active & (h == 1))
            def _():
                for part in (1, 2, 3):
                    absorb(t, part)

            @pl.when(invert & (h == 1))
            def _():
                half[...] = -nn(diag[blk, 1], diag[blk, 0])
                diag[blk, 2] = diag[blk, 2] - nt(half[...], diag[blk, 1])

            @pl.when(invert)
            def _():
                sweep(diag.at[blk, 2 * h])

            return carry

        lax.fori_loop(0, 2, part_of, 0)

        @pl.when((t == levels) & (pos == 0))
        def _():
            for part in range(4):
                root_copy(part).start()

        def each_coupling(act):
            @pl.when(odd)
            def _():
                act(0)

                @pl.when(t >= 2)
                def _():
                    act(1)

        def hand_on(slot):
            message(t - 1, 0, 1 - slot, 0, 1, 4).wait_recv()
            pair_copy(slot).start()

        each_coupling(hand_on)

        @pl.when(invert)
        def _():
            lower = nn(diag[blk, 2], half[...])
            upper = lower.T
            full[H:, H:] = -diag[blk, 2]
            full[H:, :H] = lower
            full[:H, H:] = upper
            full[:H, :H] = -diag[blk, 0] - nn(upper, half[...])

        each_coupling(lambda slot: pair_copy(slot).wait_recv())

        @pl.when(odd | (t == 0))
        def _():
            products(t, blk, step)

        @pl.when(odd)
        def _():
            wait_sent(t, blk, step)

        each_coupling(lambda slot: pair_copy(slot).wait_send())

        @pl.when(root)
        def _():
            x_root[...] = nn(d_rhs[...], full[...])

        return jnp.where(t == 0, 1, 2 * step)

    lax.fori_loop(0, levels + 2, eliminate, jnp.int32(1))

    def x_copy(there, slot, index):
        return pltpu.make_async_remote_copy(
            src_ref=x_own, dst_ref=x_in.at[slot], send_sem=x_send.at[index], recv_sem=x_recv.at[slot],
            device_id={"tm": there}, device_id_type=pl.DeviceIdType.MESH,
        )

    def x_targets(level):
        targets = []
        for lower in reversed(range(level)):
            step = 2**lower
            targets.append((pos + step, 0, 2 * lower))
            if lower > 0:
                targets.append((pos - step, 1, 2 * lower + 1))
        targets.append((pos - 1, 2, 1))
        return targets

    def start_x(level):
        for there, slot, index in x_targets(level):
            @pl.when(exists(there))
            def _(there=there, slot=slot, index=index):
                x_copy(there, slot, index).start()

    def wait_x(level):
        for there, slot, index in x_targets(level):
            @pl.when(exists(there))
            def _(there=there, slot=slot, index=index):
                x_copy(there, slot, index).wait_send()

    def first_copy(k):
        there = 2**k if k < levels - 1 else 0
        return pltpu.make_async_remote_copy(
            src_ref=x_root, dst_ref=x_in.at[0], send_sem=z_send.at[k], recv_sem=x_recv.at[0],
            device_id={"tm": there}, device_id_type=pl.DeviceIdType.MESH,
        )

    @pl.when(pos == middle)
    def _():
        for k in reversed(range(levels - 1)):
            first_copy(k).start()
        first_copy(levels - 1).start()
        x_own[...] = gain[0, 2 * N : 2 * N + 8, :] - nn(x_root[...], gain[0, 0:N, :])
        start_x(levels - 1)

    @pl.when(pos == 0)
    def _():
        x_copy(pos, 0, 0).wait_recv()
        x_own[...] = x_in[0]

    for level in reversed(range(levels - 1)):
        step = 2**level

        @pl.when(pos % (2 * step) == step)
        def _(level=level, step=step):
            side_o = next_odd_side(1, step)
            x_own[...] = gain[0, 2 * N : 2 * N + 8, :]
            for side in (1 - side_o, side_o):
                @pl.when((side == 0) | (pos + step < width))
                def _(side=side):
                    slot = side * (2 if level == 0 else 1)
                    x_copy(pos, slot, 0).wait_recv()
                    x_own[...] = x_own[...] - nn(x_in[slot], gain[0, pl.ds(pl.multiple_of(side * N, N), N), :])
            start_x(level)

    out[:, 0, :] = x_own[...]
    out[:, 1, :] = gain[1, 2 * N : 2 * N + 8, :] - nn(x_own[...], gain[1, 0:N, :])

    @pl.when(pos < width - 1)
    def _():
        @pl.when(pos % 2 == 0)
        def _():
            x_copy(pos, 2, 0).wait_recv()

        out[:, 1, :] = out[:, 1, :] - nn(x_in[2], gain[1, N : 2 * N, :])

    wait_sent(jnp.int32(0), 1, jnp.int32(1))

    @pl.when(pos == 0)
    def _():
        for part in range(4):
            root_copy(part).wait_send()

    @pl.when(pos == middle)
    def _():
        for k in range(levels):
            first_copy(k).wait_send()
        wait_x(levels - 1)

    for level in range(levels - 1):
        @pl.when(pos % (2 * 2**level) == 2**level)
        def _(level=level):
            wait_x(level)


def per_device(jacobians, damping, right_sides):
    width = lax.axis_size("tm")
    peers = lax.axis_size("rhs")
    levels = width.bit_length() - 1
    vmem = pl.BlockSpec(memory_space=pltpu.VMEM)
    return pl.pallas_call(
        functools.partial(kernel, width, peers, levels),
        out_shape=jax.ShapeDtypeStruct(right_sides.shape, F32),
        in_specs=[pl.BlockSpec(memory_space=pl.ANY)] * 3,
        out_specs=vmem,
        scratch_shapes=[
            pltpu.VMEM((2, N, N), jnp.bfloat16),
            pltpu.VMEM(damping.shape, F32),
            pltpu.VMEM(right_sides.shape, F32),
            pltpu.VMEM((2, 3, H, H), F32),
            pltpu.VMEM((2, 2 * N + 8, N), F32),
            pltpu.VMEM((H, H), F32),
            pltpu.VMEM((N, N), F32),
            pltpu.VMEM((2, 2 * N + 8, N), F32),
            pltpu.VMEM((2, 2, 3, H, H), F32),
            pltpu.VMEM((2, 2, 8, N), F32),
            pltpu.VMEM((2, H, N), F32),
            pltpu.VMEM((levels, 2, 3, H, H), F32),
            pltpu.VMEM((levels, 2, 8, N), F32),
            pltpu.VMEM((3, H, H), F32),
            pltpu.VMEM((8, N), F32),
            pltpu.VMEM((8, N), F32),
            pltpu.VMEM((8, N), F32),
            pltpu.VMEM((3, 8, N), F32),
            pltpu.SemaphoreType.DMA((3,)),
            pltpu.SemaphoreType.DMA((peers - 1,)),
            pltpu.SemaphoreType.DMA((peers - 1,)),
            pltpu.SemaphoreType.DMA((2, 2, 5)),
            pltpu.SemaphoreType.DMA((levels, 2, 4)),
            pltpu.SemaphoreType.DMA((2,)),
            pltpu.SemaphoreType.DMA((2,)),
            pltpu.SemaphoreType.DMA((2,)),
            pltpu.SemaphoreType.DMA((4,)),
            pltpu.SemaphoreType.DMA((4,)),
            pltpu.SemaphoreType.DMA((levels,)),
            pltpu.SemaphoreType.DMA((2 * levels,)),
            pltpu.SemaphoreType.DMA((3,)),
        ],
        compiler_params=pltpu.CompilerParams(
            collective_id=0, has_side_effects=True, vmem_limit_bytes=32 * 1024 * 1024
        ),
    )(jacobians, damping, right_sides)


def solution(mesh):
    in_specs = (P("tm", "rhs", None), P("tm", None), P("rhs", "tm", None))
    return jax.shard_map(
        per_device, mesh=mesh, in_specs=in_specs, out_specs=P("rhs", "tm", None), check_vma=False
    )
```

time: 178 us -> 137 us (0.77)
  Pallas kernels: 175 us -> 134 us
    pallas_call x1, Pallas kernels: 175 us -> 134 us  [per_device(): pl.pallas_call(functools.partial(kernel, width, peers, levels), out_shape...]
where the time goes in v2:
time: 137 us
  Pallas kernels  134 us (98%)
  local copies, waits for them, and re-layouts  2.76 us (2%)
    pallas_call x1, Pallas kernels, per_device(): pl.pallas_call(functools.partial(kernel, width, peers, levels), out_shape...  134 us
    unnamed x7, local copies, waits for them, and re-layouts  2.76 us

profile of v2, /device:TPU:16, one launch (start us, length us, event | category | flops | bytes accessed | tf_op | source)
XLA Modules:
  0.0 137.0 jit_solution(18212712160469256242)
XLA Ops:
  0.0 0.0 copy-start
  0.0 0.8 copy-done
  0.8 0.0 copy-start.1
  0.8 0.7 copy-done.1
  1.5 0.0 copy-start.2
  1.5 0.7 copy-done.2
  2.2 134.3 %shard_map.37 = f32[8,2,256]{2,1,0:T(2,128)S(1)} custom-call(bf16[2,32,256]{2,1,0:T(8,128)(2,1)S(1)} %copy-done, f32[2,256]{1,0:T(2,128)S(1)} %copy-done.2, f32[8,2,256]{2,1,0:T(2,128)S(1)} %copy-done.1), custom_call_target="tpu_custom_call" | custom-call | tf_op jit(solution)/shard_map/pallas_call | solution.py:478
  136.4 0.6 copy.5
Async XLA Ops:
  0.0 0.8 copy-start
  0.8 0.7 copy-start.1
  1.5 0.7 copy-start.2

commit v3 on v2

--- a/solution.py
+++ b/solution.py
@@ -93,16 +93,14 @@
     width, peers, levels,
     jac, damp, rhs, out,
     whole, damp_in, rhs_in, diag, links, half, full, gain, t_out, r_out, c_out, t_in, r_in,
-    d_in, d_rhs, x_root, x_own, x_in,
-    i_sem, j_send, j_recv, m_send, t_recv, a_recv, p_send, p_recv, d_send, d_recv, z_send, x_send, x_recv,
+    d_in, d_rhs, map_o, map_n, x_root, x_own, x_o, x_in,
+    i_sem, j_send, j_recv, m_send, t_recv, a_recv, p_send, p_recv, d_send, d_recv, g_send, g_recv, z_send, x_send, x_recv,
 ):
     pos = lax.axis_index("tm")
     me = lax.axis_index("rhs")
     middle = width // 2
+    tops = list(range(levels - 2, -1, -2))
     core = me % 2
-
-    def is_multiple(step):
-        return pos % step == 0
 
     depth = jac.shape[1]
     mine = pl.ds(pl.multiple_of(me * depth, depth), depth)
@@ -118,12 +116,9 @@
     count = peers - 1
     for d in range(1, peers):
         pl.semaphore_signal(barrier, inc=1, device_id={"rhs": (me + d) % peers}, device_id_type=pl.DeviceIdType.MESH)
-    partners = [((pos + sign * 2**k), is_multiple(2**k)) for k in range(levels) for sign in (-1, 1)]
-    for k in range(levels - 2):
-        partners.append((jnp.int32(2**k), pos == middle))
-        partners.append((jnp.int32(middle), pos == 2**k))
-    for there, holds in partners:
-        partner = holds & (there >= 0) & (there < width)
+    for sign in (-1, 1):
+        there = pos + sign
+        partner = (there >= 0) & (there < width)
         count = count + partner.astype(jnp.int32)
 
         @pl.when(partner)
@@ -131,33 +126,36 @@
             pl.semaphore_signal(barrier, inc=1, device_id={"tm": there}, device_id_type=pl.DeviceIdType.MESH)
     pl.semaphore_wait(barrier, count)
 
-    def row_copy(d):
+    def row_copy(k, d):
         return pltpu.make_async_remote_copy(
-            src_ref=jac, dst_ref=whole.at[:, mine, :], send_sem=j_send.at[d - 1], recv_sem=j_recv.at[d - 1],
+            src_ref=jac.at[k], dst_ref=whole.at[k, mine, :], send_sem=j_send.at[k, d - 1], recv_sem=j_recv.at[k, d - 1],
             device_id={"rhs": (me + d) % peers}, device_id_type=pl.DeviceIdType.MESH,
         )
 
-    for d in range(1, peers):
-        row_copy(d).start()
+    for k in (1, 0):
+        for d in range(1, peers):
+            row_copy(k, d).start()
     for load in loads:
         load.wait()
-    for d in range(1, peers):
-        row_copy(d).wait()
-
-    on_diag = lax.broadcasted_iota(jnp.int32, (N, N), 0) == lax.broadcasted_iota(jnp.int32, (N, N), 1)
-    first = jnp.where(pos > 0, 1.0, 0.0).astype(F32)
-    for k in range(2):
+
+    def local_block(k):
+        for d in range(1, peers):
+            row_copy(k, d).wait()
+        on_diag = lax.broadcasted_iota(jnp.int32, (N, N), 0) == lax.broadcasted_iota(jnp.int32, (N, N), 1)
         block = lax.dot_general(whole[k], whole[k], (((0,), (0,)), ((), ())), preferred_element_type=F32)
-        extra = damp_in[k : k + 1, :] + (first if k == 0 else 1.0)
+        extra = damp_in[k : k + 1, :] + (jnp.where(pos > 0, 1.0, 0.0).astype(F32) if k == 0 else 1.0)
         block = block + jnp.where(on_diag, jnp.broadcast_to(extra, (N, N)), 0.0)
         diag[k, 0] = block[:H, :H]
         diag[k, 1] = block[H:, :H]
         diag[k, 2] = block[H:, H:]
-    last = jnp.where(pos < width - 1, 1.0, 0.0).astype(F32)
-    links[1, 0:N, :] = -whole[0].astype(F32).T
-    links[1, N : 2 * N, :] = -whole[1].astype(F32) * last
-    for k in range(2):
         links[k, 2 * N : 2 * N + 8, :] = rhs_in[:, k, :]
+        if k == 0:
+            links[1, 0:N, :] = -whole[0].astype(F32).T
+        else:
+            last = jnp.where(pos < width - 1, 1.0, 0.0).astype(F32)
+            links[1, N : 2 * N, :] = -whole[1].astype(F32) * last
+
+    local_block(1)
 
     def coupling_half(slot, which):
         return links.at[0, pl.ds(pl.multiple_of(slot * N + which * H, H), H), :]
@@ -298,6 +296,17 @@
                 for part in range(5 - place):
                     message(t, blk, side, place, hop, part).wait_send()
 
+    def each_map(level, act):
+        for sign in (-1, 1) if level > 0 else (-1,):
+            there = pos + sign * (2**level // 2 if level > 0 else 1)
+            act(
+                pltpu.make_async_remote_copy(
+                    src_ref=gain.at[0], dst_ref=map_o if level > 0 else map_n,
+                    send_sem=g_send.at[0 if sign < 0 else 1], recv_sem=g_recv.at[0 if level > 0 else 1],
+                    device_id={"tm": there}, device_id_type=pl.DeviceIdType.MESH,
+                )
+            )
+
     def eliminate(t, step):
         blk = jnp.where(t == 0, 1, 0)
         active = (t >= 1) & (t <= levels) & (pos % step == 0)
@@ -306,6 +315,10 @@
         invert = (t == 0) | odd | root
 
         def part_of(h, carry):
+            @pl.when((t == 0) & (h == 1))
+            def _():
+                local_block(0)
+
             @pl.when(active & (h == 0))
             def _():
                 absorb(t, 0)
@@ -363,6 +376,11 @@
         def _():
             products(t, blk, step)
 
+        for level in tops:
+            @pl.when(odd & (t == level + 1))
+            def _(level=level):
+                each_map(level, lambda copy: copy.start())
+
         @pl.when(odd)
         def _():
             wait_sent(t, blk, step)
@@ -377,79 +395,128 @@
 
     lax.fori_loop(0, levels + 2, eliminate, jnp.int32(1))
 
-    def x_copy(there, slot, index):
+    def x_copy(src, there, slot, index):
         return pltpu.make_async_remote_copy(
-            src_ref=x_own, dst_ref=x_in.at[slot], send_sem=x_send.at[index], recv_sem=x_recv.at[slot],
+            src_ref=src, dst_ref=x_in.at[slot], send_sem=x_send.at[index], recv_sem=x_recv.at[slot],
             device_id={"tm": there}, device_id_type=pl.DeviceIdType.MESH,
         )
 
-    def x_targets(level):
-        targets = []
-        for lower in reversed(range(level)):
-            step = 2**lower
-            targets.append((pos + step, 0, 2 * lower))
-            if lower > 0:
-                targets.append((pos - step, 1, 2 * lower + 1))
-        targets.append((pos - 1, 2, 1))
-        return targets
-
-    def start_x(level):
-        for there, slot, index in x_targets(level):
-            @pl.when(exists(there))
-            def _(there=there, slot=slot, index=index):
-                x_copy(there, slot, index).start()
-
-    def wait_x(level):
-        for there, slot, index in x_targets(level):
-            @pl.when(exists(there))
-            def _(there=there, slot=slot, index=index):
-                x_copy(there, slot, index).wait_send()
-
-    def first_copy(k):
-        there = 2**k if k < levels - 1 else 0
+    def wait_for(slot):
+        x_copy(x_own, pos, slot, 0).wait_recv()
+
+    def group_targets(at, top):
+        if top == 0:
+            return [(at + 1, 0), (at - 1, 1), (at - 2, 3)]
+        reach = 2**top
+        near = [(at + reach, 0), (at - reach, 1)]
+        half_reach = reach // 2
+        return near + [
+            (at + half_reach, 0), (at - half_reach, 1), (at + 3 * half_reach, 2), (at - 3 * half_reach, 2),
+        ]
+
+    def each_target(src, at, level, base, act):
+        index = base
+        for top in tops:
+            if top <= level:
+                for there, slot in group_targets(at, top):
+                    @pl.when(exists(there))
+                    def _(there=there, slot=slot, index=index):
+                        act(x_copy(src, there, slot, index))
+                    index += 1
+
+    def start(copy):
+        copy.start()
+
+    def sent(copy):
+        copy.wait_send()
+
+    def term(x, of, side):
+        return nn(x, of[pl.ds(pl.multiple_of(side * N, N), N), :])
+
+    own_map = gain.at[0]
+
+    def root_targets(act):
+        each_target(x_root, 0, levels - 2, 0, act)
+
+    def home_copy():
         return pltpu.make_async_remote_copy(
-            src_ref=x_root, dst_ref=x_in.at[0], send_sem=z_send.at[k], recv_sem=x_recv.at[0],
-            device_id={"tm": there}, device_id_type=pl.DeviceIdType.MESH,
+            src_ref=x_root, dst_ref=x_in.at[0], send_sem=z_send, recv_sem=x_recv.at[0],
+            device_id={"tm": 0}, device_id_type=pl.DeviceIdType.MESH,
         )
 
     @pl.when(pos == middle)
     def _():
-        for k in reversed(range(levels - 1)):
-            first_copy(k).start()
-        first_copy(levels - 1).start()
+        root_targets(start)
+        home_copy().start()
         x_own[...] = gain[0, 2 * N : 2 * N + 8, :] - nn(x_root[...], gain[0, 0:N, :])
-        start_x(levels - 1)
+        each_target(x_own, middle, levels - 2, 24, start)
 
     @pl.when(pos == 0)
     def _():
-        x_copy(pos, 0, 0).wait_recv()
+        wait_for(0)
         x_own[...] = x_in[0]
 
     for level in reversed(range(levels - 1)):
         step = 2**level
+        top = [t for t in tops if level in (t, t - 1)][0]
 
         @pl.when(pos % (2 * step) == step)
-        def _(level=level, step=step):
-            side_o = next_odd_side(1, step)
+        def _(level=level, step=step, top=top):
+            upper = pos + step < width
             x_own[...] = gain[0, 2 * N : 2 * N + 8, :]
-            for side in (1 - side_o, side_o):
-                @pl.when((side == 0) | (pos + step < width))
-                def _(side=side):
-                    slot = side * (2 if level == 0 else 1)
-                    x_copy(pos, slot, 0).wait_recv()
-                    x_own[...] = x_own[...] - nn(x_in[slot], gain[0, pl.ds(pl.multiple_of(side * N, N), N), :])
-            start_x(level)
+            if level == top:
+                wait_for(0)
+                x_own[...] = x_own[...] - term(x_in[0], own_map, 0)
+
+                @pl.when(upper)
+                def _():
+                    wait_for(1)
+                    x_own[...] = x_own[...] - term(x_in[1], own_map, 1)
+            else:
+                side_o = next_odd_side(1, step)
+                side_e = 1 - side_o
+                each_end = ((side_e, side_e, exists(pos + step * (2 * side_e - 1))),
+                            (side_o, 2, exists(pos + 3 * step * (2 * side_o - 1))))
+                pltpu.make_async_remote_copy(
+                    src_ref=own_map, dst_ref=map_o, send_sem=g_send.at[0], recv_sem=g_recv.at[0],
+                    device_id={"tm": pos}, device_id_type=pl.DeviceIdType.MESH,
+                ).wait_recv()
+                x_o[...] = map_o[2 * N : 2 * N + 8, :]
+                for side, slot, there in each_end:
+                    @pl.when(there)
+                    def _(side=side, slot=slot):
+                        wait_for(slot)
+                        x_o[...] = x_o[...] - term(x_in[slot], map_o, side)
+
+                @pl.when(exists(pos + step * (2 * side_e - 1)))
+                def _():
+                    x_own[...] = x_own[...] - term(x_in[side_e], own_map, side_e)
+
+                x_own[...] = x_own[...] - term(x_o[...], own_map, side_o)
+            if level > 0:
+                each_target(x_own, pos, top - 1 if level == top else top - 2, 0, start)
 
     out[:, 0, :] = x_own[...]
     out[:, 1, :] = gain[1, 2 * N : 2 * N + 8, :] - nn(x_own[...], gain[1, 0:N, :])
 
-    @pl.when(pos < width - 1)
+    @pl.when(pos % 2 == 0)
     def _():
-        @pl.when(pos % 2 == 0)
-        def _():
-            x_copy(pos, 2, 0).wait_recv()
-
-        out[:, 1, :] = out[:, 1, :] - nn(x_in[2], gain[1, N : 2 * N, :])
+        pltpu.make_async_remote_copy(
+            src_ref=own_map, dst_ref=map_n, send_sem=g_send.at[0], recv_sem=g_recv.at[1],
+            device_id={"tm": pos}, device_id_type=pl.DeviceIdType.MESH,
+        ).wait_recv()
+        x_o[...] = map_n[2 * N : 2 * N + 8, :] - term(x_own[...], map_n, 0)
+
+        @pl.when(pos + 2 < width)
+        def _():
+            wait_for(3)
+            x_o[...] = x_o[...] - term(x_in[3], map_n, 1)
+
+        out[:, 1, :] = out[:, 1, :] - nn(x_o[...], gain[1, N : 2 * N, :])
+
+    @pl.when((pos % 2 == 1) & (pos < width - 1))
+    def _():
+        out[:, 1, :] = out[:, 1, :] - nn(x_in[1], gain[1, N : 2 * N, :])
 
     wait_sent(jnp.int32(0), 1, jnp.int32(1))
 
@@ -460,14 +527,19 @@
 
     @pl.when(pos == middle)
     def _():
-        for k in range(levels):
-            first_copy(k).wait_send()
-        wait_x(levels - 1)
+        root_targets(sent)
+        home_copy().wait_send()
+        each_target(x_own, middle, levels - 2, 24, sent)
 
     for level in range(levels - 1):
+        top = [t for t in tops if level in (t, t - 1)][0]
+
         @pl.when(pos % (2 * 2**level) == 2**level)
-        def _(level=level):
-            wait_x(level)
+        def _(level=level, top=top):
+            if level == top:
+                each_map(level, sent)
+            if level > 0:
+                each_target(x_own, pos, top - 1 if level == top else top - 2, 0, sent)
 
 
 def per_device(jacobians, damping, right_sides):
@@ -496,12 +568,15 @@
             pltpu.VMEM((levels, 2, 8, N), F32),
             pltpu.VMEM((3, H, H), F32),
             pltpu.VMEM((8, N), F32),
+            pltpu.VMEM((2 * N + 8, N), F32),
+            pltpu.VMEM((2 * N + 8, N), F32),
             pltpu.VMEM((8, N), F32),
             pltpu.VMEM((8, N), F32),
-            pltpu.VMEM((3, 8, N), F32),
+            pltpu.VMEM((8, N), F32),
+            pltpu.VMEM((4, 8, N), F32),
             pltpu.SemaphoreType.DMA((3,)),
-            pltpu.SemaphoreType.DMA((peers - 1,)),
-            pltpu.SemaphoreType.DMA((peers - 1,)),
+            pltpu.SemaphoreType.DMA((2, peers - 1)),
+            pltpu.SemaphoreType.DMA((2, peers - 1)),
             pltpu.SemaphoreType.DMA((2, 2, 5)),
             pltpu.SemaphoreType.DMA((levels, 2, 4)),
             pltpu.SemaphoreType.DMA((2,)),
@@ -509,9 +584,11 @@
             pltpu.SemaphoreType.DMA((2,)),
             pltpu.SemaphoreType.DMA((4,)),
             pltpu.SemaphoreType.DMA((4,)),
-            pltpu.SemaphoreType.DMA((levels,)),
-            pltpu.SemaphoreType.DMA((2 * levels,)),
-            pltpu.SemaphoreType.DMA((3,)),
+            pltpu.SemaphoreType.DMA((2,)),
+            pltpu.SemaphoreType.DMA((2,)),
+            pltpu.SemaphoreType.DMA(()),
+            pltpu.SemaphoreType.DMA((48,)),
+            pltpu.SemaphoreType.DMA((4,)),
         ],
         compiler_params=pltpu.CompilerParams(
             collective_id=0, has_side_effects=True, vmem_limit_bytes=32 * 1024 * 1024

time: 137 us -> 129 us (0.942)
  Pallas kernels: 134 us -> 126 us
    pallas_call x1, Pallas kernels: 134 us -> 126 us  [per_device(): pl.pallas_call(functools.partial(kernel, width, peers, levels), out_shape...]
where the time goes in v3:
time: 129 us
  Pallas kernels  126 us (98%)
  local copies, waits for them, and re-layouts  2.76 us (2%)
    pallas_call x1, Pallas kernels, per_device(): pl.pallas_call(functools.partial(kernel, width, peers, levels), out_shape...  126 us
    unnamed x7, local copies, waits for them, and re-layouts  2.76 us

profile of v3, /device:TPU:16, one launch (start us, length us, event | category | flops | bytes accessed | tf_op | source)
XLA Modules:
  0.0 129.1 jit_solution(8833657232395749944)
XLA Ops:
  0.0 0.0 copy-start
  0.0 0.8 copy-done
  0.8 0.0 copy-start.1
  0.8 0.7 copy-done.1
  1.5 0.0 copy-start.2
  1.5 0.7 copy-done.2
  2.2 126.3 %shard_map.37 = f32[8,2,256]{2,1,0:T(2,128)S(1)} custom-call(bf16[2,32,256]{2,1,0:T(8,128)(2,1)S(1)} %copy-done, f32[2,256]{1,0:T(2,128)S(1)} %copy-done.2, f32[8,2,256]{2,1,0:T(2,128)S(1)} %copy-done.1), custom_call_target="tpu_custom_call" | custom-call | tf_op jit(solution)/shard_map/pallas_call | solution.py:550
  128.4 0.6 copy.5
Async XLA Ops:
  0.0 0.8 copy-start
  0.8 0.7 copy-start.1
  1.5 0.7 copy-start.2

commit v4 on v3

--- a/solution.py
+++ b/solution.py
@@ -19,6 +19,35 @@
 
 def nt(a, b):
     return lax.dot_general(a, b, (((1,), (1,)), ((), ())), precision=HIGHEST, preferred_element_type=F32)
+
+
+def in_parts(x, count):
+    parts = []
+    for _ in range(count):
+        parts.append(x.astype(jnp.bfloat16))
+        x = x - parts[-1].astype(F32)
+    return parts
+
+
+def joined(a, b, order, axis):
+    left = jnp.concatenate([a[i] for i, _ in order], axis=1)
+    right = jnp.concatenate([b[j] for _, j in order], axis=axis)
+    return lax.dot_general(left, right, (((1,), (axis,)), ((), ())), preferred_element_type=F32)
+
+
+SIX = ((2, 0), (0, 2), (1, 1), (1, 0), (0, 1), (0, 0))
+
+
+def nn6(a, b):
+    return joined(in_parts(a, 3), in_parts(b, 3), SIX, 0)
+
+
+def nt6(a, b):
+    return joined(in_parts(a, 3), in_parts(b, 3), SIX, 1)
+
+
+def thrice(a, b):
+    return joined(in_parts(a, 2), in_parts(b, 2), ((1, 0), (0, 1), (0, 0)), 0)
 
 
 def spread(x):
@@ -94,7 +123,7 @@
     jac, damp, rhs, out,
     whole, damp_in, rhs_in, diag, links, half, full, gain, t_out, r_out, c_out, t_in, r_in,
     d_in, d_rhs, map_o, map_n, x_root, x_own, x_o, x_in,
-    i_sem, j_send, j_recv, m_send, t_recv, a_recv, p_send, p_recv, d_send, d_recv, g_send, g_recv, z_send, x_send, x_recv,
+    i_sem, j_send, j_recv, m_send, t_recv, a_recv, p_send, p_recv, d_send, d_recv, token, g_send, g_recv, z_send, x_send, x_recv,
 ):
     pos = lax.axis_index("tm")
     me = lax.axis_index("rhs")
@@ -178,16 +207,25 @@
 
     def message(t, blk, side, place, hop, part):
         slot = 1 - side
+        past = (t == levels - 1) & (pos == middle // 2) & (side == 0)
+        at, cell = jnp.where(past, 0, t), jnp.where(past, 1, slot)
         if part < 3:
-            src, dst, sem = t_out.at[blk, side, part], t_in.at[t, slot, part], t_recv.at[t, slot, part]
+            src, dst, sem = t_out.at[blk, side, part], t_in.at[at, cell, part], t_recv.at[at, cell, part]
         elif part == 3:
-            src, dst, sem = r_out.at[blk, side], r_in.at[t, slot], t_recv.at[t, slot, 3]
+            src, dst, sem = r_out.at[blk, side], r_in.at[at, cell], t_recv.at[at, cell, 3]
         else:
             dst = coupling_half(slot, core)
             src, sem = c_out.at[blk], a_recv.at[slot]
         return pltpu.make_async_remote_copy(
             src_ref=src, dst_ref=dst, send_sem=m_send.at[blk, place, part], recv_sem=sem,
-            device_id={"tm": pos + hop * (2 * side - 1)}, device_id_type=pl.DeviceIdType.MESH,
+            device_id={"tm": jnp.where(past, middle, pos + hop * (2 * side - 1))}, device_id_type=pl.DeviceIdType.MESH,
+        )
+
+    def straight(part):
+        dst = t_in.at[0, 1, part] if part < 3 else r_in.at[0, 1]
+        return pltpu.make_async_remote_copy(
+            src_ref=dst, dst_ref=dst, send_sem=m_send.at[0, 0, part], recv_sem=t_recv.at[0, 1, part],
+            device_id={"tm": pos}, device_id_type=pl.DeviceIdType.MESH,
         )
 
     def exists(there):
@@ -279,9 +317,10 @@
         def _():
             for part in range(4):
                 root_copy(part).wait_recv()
+                straight(part).wait_recv()
             for part in range(3):
-                diag[0, part] = d_in[part] - t_out[blk, 0, part]
-            d_rhs[...] = d_rhs[...] - r_out[blk, 0]
+                diag[0, part] = d_in[part] - t_in[0, 1, part] - t_out[blk, 0, part]
+            d_rhs[...] = d_rhs[...] - r_in[0, 1] - r_out[blk, 0]
 
     def wait_sent(t, blk, step):
         side_o = next_odd_side(t, step)
@@ -309,7 +348,7 @@
 
     def eliminate(t, step):
         blk = jnp.where(t == 0, 1, 0)
-        active = (t >= 1) & (t <= levels) & (pos % step == 0)
+        active = (t >= 1) & (t <= levels) & (pos % step == 0) & ((t < levels) | (pos > 0))
         odd = active & (pos // step % 2 == 1)
         root = (t == levels + 1) & (pos == middle)
         invert = (t == 0) | odd | root
@@ -323,6 +362,10 @@
             def _():
                 absorb(t, 0)
 
+            @pl.when(active & (h == 0) & (t == levels - 1) & (pos == middle // 2))
+            def _():
+                pl.semaphore_signal(token, inc=1, device_id={"tm": 0}, device_id_type=pl.DeviceIdType.MESH)
+
             @pl.when(active & (h == 1))
             def _():
                 for part in (1, 2, 3):
@@ -330,8 +373,8 @@
 
             @pl.when(invert & (h == 1))
             def _():
-                half[...] = -nn(diag[blk, 1], diag[blk, 0])
-                diag[blk, 2] = diag[blk, 2] - nt(half[...], diag[blk, 1])
+                half[...] = -nn6(diag[blk, 1], diag[blk, 0])
+                diag[blk, 2] = diag[blk, 2] - nt6(half[...], diag[blk, 1])
 
             @pl.when(invert)
             def _():
@@ -341,8 +384,9 @@
 
         lax.fori_loop(0, 2, part_of, 0)
 
-        @pl.when((t == levels) & (pos == 0))
-        def _():
+        @pl.when((t == levels - 1) & (pos == 0))
+        def _():
+            pl.semaphore_wait(token, 1)
             for part in range(4):
                 root_copy(part).start()
 
@@ -363,12 +407,12 @@
 
         @pl.when(invert)
         def _():
-            lower = nn(diag[blk, 2], half[...])
+            lower = nn6(diag[blk, 2], half[...])
             upper = lower.T
             full[H:, H:] = -diag[blk, 2]
             full[H:, :H] = lower
             full[:H, H:] = upper
-            full[:H, :H] = -diag[blk, 0] - nn(upper, half[...])
+            full[:H, :H] = -diag[blk, 0] - nn6(upper, half[...])
 
         each_coupling(lambda slot: pair_copy(slot).wait_recv())
 
@@ -414,15 +458,17 @@
             (at + half_reach, 0), (at - half_reach, 1), (at + 3 * half_reach, 2), (at - 3 * half_reach, 2),
         ]
 
-    def each_target(src, at, level, base, act):
-        index = base
-        for top in tops:
-            if top <= level:
-                for there, slot in group_targets(at, top):
-                    @pl.when(exists(there))
-                    def _(there=there, slot=slot, index=index):
-                        act(x_copy(src, there, slot, index))
-                    index += 1
+    def each_target(src, at, group_tops, base, act):
+        for top in group_tops:
+            index = base + 6 * tops.index(top)
+            for there, slot in group_targets(at, top):
+                @pl.when(exists(there))
+                def _(there=there, slot=slot, index=index):
+                    act(x_copy(src, there, slot, index))
+                index += 1
+
+    def below(level):
+        return [top for top in tops if top < level]
 
     def start(copy):
         copy.start()
@@ -430,13 +476,20 @@
     def sent(copy):
         copy.wait_send()
 
-    def term(x, of, side):
-        return nn(x, of[pl.ds(pl.multiple_of(side * N, N), N), :])
+    def take(slot, there):
+        @pl.when(there)
+        def _():
+            wait_for(slot)
+
+        @pl.when(jnp.logical_not(there))
+        def _():
+            x_in[slot] = jnp.zeros((8, N), F32)
+
+    def solved(of, lower, upper):
+        ends = jnp.concatenate([lower, upper], axis=1)
+        return of[2 * N : 2 * N + 8, :] - thrice(ends, of[0 : 2 * N, :])
 
     own_map = gain.at[0]
-
-    def root_targets(act):
-        each_target(x_root, 0, levels - 2, 0, act)
 
     def home_copy():
         return pltpu.make_async_remote_copy(
@@ -446,10 +499,12 @@
 
     @pl.when(pos == middle)
     def _():
-        root_targets(start)
+        each_target(x_root, 0, tops[:1], 0, start)
+        x_own[...] = gain[0, 2 * N : 2 * N + 8, :] - thrice(x_root[...], gain[0, 0:N, :])
+        each_target(x_own, middle, tops[:1], 24, start)
+        each_target(x_root, 0, tops[1:], 0, start)
+        each_target(x_own, middle, tops[1:], 24, start)
         home_copy().start()
-        x_own[...] = gain[0, 2 * N : 2 * N + 8, :] - nn(x_root[...], gain[0, 0:N, :])
-        each_target(x_own, middle, levels - 2, 24, start)
 
     @pl.when(pos == 0)
     def _():
@@ -462,42 +517,27 @@
 
         @pl.when(pos % (2 * step) == step)
         def _(level=level, step=step, top=top):
-            upper = pos + step < width
-            x_own[...] = gain[0, 2 * N : 2 * N + 8, :]
             if level == top:
-                wait_for(0)
-                x_own[...] = x_own[...] - term(x_in[0], own_map, 0)
-
-                @pl.when(upper)
-                def _():
-                    wait_for(1)
-                    x_own[...] = x_own[...] - term(x_in[1], own_map, 1)
+                take(0, pos >= 0)
+                take(1, pos + step < width)
+                x_own[...] = solved(own_map, x_in[0], x_in[1])
             else:
                 side_o = next_odd_side(1, step)
                 side_e = 1 - side_o
-                each_end = ((side_e, side_e, exists(pos + step * (2 * side_e - 1))),
-                            (side_o, 2, exists(pos + 3 * step * (2 * side_o - 1))))
                 pltpu.make_async_remote_copy(
                     src_ref=own_map, dst_ref=map_o, send_sem=g_send.at[0], recv_sem=g_recv.at[0],
                     device_id={"tm": pos}, device_id_type=pl.DeviceIdType.MESH,
                 ).wait_recv()
-                x_o[...] = map_o[2 * N : 2 * N + 8, :]
-                for side, slot, there in each_end:
-                    @pl.when(there)
-                    def _(side=side, slot=slot):
-                        wait_for(slot)
-                        x_o[...] = x_o[...] - term(x_in[slot], map_o, side)
-
-                @pl.when(exists(pos + step * (2 * side_e - 1)))
-                def _():
-                    x_own[...] = x_own[...] - term(x_in[side_e], own_map, side_e)
-
-                x_own[...] = x_own[...] - term(x_o[...], own_map, side_o)
+                take(side_e, exists(pos + step * (2 * side_e - 1)))
+                take(2, exists(pos + 3 * step * (2 * side_o - 1)))
+                near, far = x_in[side_e], x_in[2]
+                flip = side_e == 1
+                between = solved(map_o, jnp.where(flip, far, near), jnp.where(flip, near, far))
+                x_own[...] = solved(own_map, jnp.where(flip, between, near), jnp.where(flip, near, between))
             if level > 0:
-                each_target(x_own, pos, top - 1 if level == top else top - 2, 0, start)
+                each_target(x_own, pos, below(level if level == top else top), 0, start)
 
     out[:, 0, :] = x_own[...]
-    out[:, 1, :] = gain[1, 2 * N : 2 * N + 8, :] - nn(x_own[...], gain[1, 0:N, :])
 
     @pl.when(pos % 2 == 0)
     def _():
@@ -505,18 +545,12 @@
             src_ref=own_map, dst_ref=map_n, send_sem=g_send.at[0], recv_sem=g_recv.at[1],
             device_id={"tm": pos}, device_id_type=pl.DeviceIdType.MESH,
         ).wait_recv()
-        x_o[...] = map_n[2 * N : 2 * N + 8, :] - term(x_own[...], map_n, 0)
-
-        @pl.when(pos + 2 < width)
-        def _():
-            wait_for(3)
-            x_o[...] = x_o[...] - term(x_in[3], map_n, 1)
-
-        out[:, 1, :] = out[:, 1, :] - nn(x_o[...], gain[1, N : 2 * N, :])
-
-    @pl.when((pos % 2 == 1) & (pos < width - 1))
+        take(3, pos + 2 < width)
+        out[:, 1, :] = solved(gain.at[1], x_own[...], solved(map_n, x_own[...], x_in[3]))
+
+    @pl.when(pos % 2 == 1)
     def _():
-        out[:, 1, :] = out[:, 1, :] - nn(x_in[1], gain[1, N : 2 * N, :])
+        out[:, 1, :] = solved(gain.at[1], x_own[...], x_in[1])
 
     wait_sent(jnp.int32(0), 1, jnp.int32(1))
 
@@ -527,9 +561,9 @@
 
     @pl.when(pos == middle)
     def _():
-        root_targets(sent)
+        each_target(x_root, 0, tops, 0, sent)
+        each_target(x_own, middle, tops, 24, sent)
         home_copy().wait_send()
-        each_target(x_own, middle, levels - 2, 24, sent)
 
     for level in range(levels - 1):
         top = [t for t in tops if level in (t, t - 1)][0]
@@ -539,7 +573,7 @@
             if level == top:
                 each_map(level, sent)
             if level > 0:
-                each_target(x_own, pos, top - 1 if level == top else top - 2, 0, sent)
+                each_target(x_own, pos, below(level if level == top else top), 0, sent)
 
 
 def per_device(jacobians, damping, right_sides):
@@ -584,6 +618,7 @@
             pltpu.SemaphoreType.DMA((2,)),
             pltpu.SemaphoreType.DMA((4,)),
             pltpu.SemaphoreType.DMA((4,)),
+            pltpu.SemaphoreType.REGULAR,
             pltpu.SemaphoreType.DMA((2,)),
             pltpu.SemaphoreType.DMA((2,)),
             pltpu.SemaphoreType.DMA(()),

time: 129 us -> 128 us (level)
    pallas_call x1, Pallas kernels: 126 us -> 125 us  [per_device(): pl.pallas_call(functools.partial(kernel, width, peers, levels), out_shape...]
where the time goes in v4:
time: 128 us
  Pallas kernels  125 us (98%)
  local copies, waits for them, and re-layouts  2.76 us (2%)
    pallas_call x1, Pallas kernels, per_device(): pl.pallas_call(functools.partial(kernel, width, peers, levels), out_shape...  125 us
    unnamed x7, local copies, waits for them, and re-layouts  2.76 us

profile of v4, /device:TPU:16, one launch (start us, length us, event | category | flops | bytes accessed | tf_op | source)
XLA Modules:
  0.0 127.5 jit_solution(2763012820540281187)
XLA Ops:
  0.0 0.0 copy-start
  0.0 0.8 copy-done
  0.8 0.0 copy-start.1
  0.8 0.7 copy-done.1
  1.5 0.0 copy-start.2
  1.5 0.7 copy-done.2
  2.2 124.8 %shard_map.37 = f32[8,2,256]{2,1,0:T(2,128)S(1)} custom-call(bf16[2,32,256]{2,1,0:T(8,128)(2,1)S(1)} %copy-done, f32[2,256]{1,0:T(2,128)S(1)} %copy-done.2, f32[8,2,256]{2,1,0:T(2,128)S(1)} %copy-done.1), custom_call_target="tpu_custom_call" | custom-call | tf_op jit(solution)/shard_map/pallas_call | solution.py:584
  126.9 0.6 copy.5
Async XLA Ops:
  0.0 0.8 copy-start
  0.8 0.7 copy-start.1
  1.5 0.7 copy-start.2

commit v5 on v4

--- a/solution.py
+++ b/solution.py
@@ -70,17 +70,17 @@
         guess = pl.reciprocal(det, approx=True)
         mend = 2.0 - det * guess
         is_a, is_b = sub == a, sub == b
-        part_a = jnp.where(is_a, -bb, jnp.where(is_b, ab, bb * cols[a] - ab * cols[b])) * guess
-        part_b = jnp.where(is_a, ab, jnp.where(is_b, -aa, aa * cols[b] - ab * cols[a])) * guess
+        part_a = jnp.where(is_a, -bb, jnp.where(is_b, ab, bb * cols[a] - ab * cols[b]))
+        part_b = jnp.where(is_a, ab, jnp.where(is_b, -aa, aa * cols[b] - ab * cols[a]))
         new = []
         for j in range(8):
             if j == a:
-                new.append(part_a * mend)
+                new.append(part_a * guess * mend)
             elif j == b:
-                new.append(part_b * mend)
+                new.append(part_b * guess * mend)
             else:
                 kept = jnp.where(is_a | is_b, 0.0, cols[j])
-                new.append(kept - (part_a * row_a[j] + part_b * row_b[j]) * mend)
+                new.append(kept - (part_a * row_a[j] + part_b * row_b[j]) * guess * mend)
         cols = new
     return cols
 

time: 128 us -> 127 us (level)
  no operation moved by 1% of the time
where the time goes in v5:
time: 127 us
  Pallas kernels  124 us (98%)
  local copies, waits for them, and re-layouts  2.76 us (2%)
    pallas_call x1, Pallas kernels, per_device(): pl.pallas_call(functools.partial(kernel, width, peers, levels), out_shape...  124 us
    unnamed x7, local copies, waits for them, and re-layouts  2.76 us

profile of v5, /device:TPU:16, one launch (start us, length us, event | category | flops | bytes accessed | tf_op | source)
XLA Modules:
  0.0 126.8 jit_solution(1383953837852030048)
XLA Ops:
  0.0 0.0 copy-start
  0.0 0.8 copy-done
  0.8 0.0 copy-start.1
  0.8 0.7 copy-done.1
  1.5 0.0 copy-start.2
  1.5 0.7 copy-done.2
  2.2 124.0 %shard_map.37 = f32[8,2,256]{2,1,0:T(2,128)S(1)} custom-call(bf16[2,32,256]{2,1,0:T(8,128)(2,1)S(1)} %copy-done, f32[2,256]{1,0:T(2,128)S(1)} %copy-done.2, f32[8,2,256]{2,1,0:T(2,128)S(1)} %copy-done.1), custom_call_target="tpu_custom_call" | custom-call | tf_op jit(solution)/shard_map/pallas_call | solution.py:584
  126.1 0.6 copy.5
Async XLA Ops:
  0.0 0.8 copy-start
  0.8 0.7 copy-start.1
  1.5 0.7 copy-start.2
